TPU v7x, 128 devices: a whole 4x4x4 slice. The times are simulated.
128 devices in a mesh: dp: 8 (over z, core), label: 16 (over x, y).
Axes of the slice: x: 4, y: 4, z: 4, core: 2. Of those that a mesh axis runs over, the one named last changes fastest.
Arguments:
- features: bfloat16 [262144, 768], P(('dp', 'label')), may hold values from -6 to 6
- inst_ids: int32 [2048, 4], P(('dp', 'label')), may hold values from 0 to 15
- lab_ids: int32 [2048, 4], P(('dp', 'label')), may hold values from 0 to 15
- counts: int32 [2048], P(('dp', 'label')), may hold values from 0 to 4, as said below
- block_bits: int32 [2048, 4, 128, 128], P(('dp', 'label')), may hold values 0 or 1
- centroids: bfloat16 [2048, 768], P('label'), may hold values from -40 to 40
Outputs:
- label_embed: bfloat16 [32768, 768], P(('dp', 'label'))
- membership: bfloat16 [32768, 2048], P(('dp', 'label'))
- targets: bfloat16 [262144, 768], P(('dp', 'label'))
Inputs may be any that keep to these rules, and one draw needn't show every extreme that they name: `lab_ids`: label block within the slot's label column. `counts`: in every draw one label column has all 4 slots used on every device.
All inputs are finite; a program needn't handle non-finite values. No bound on the sum of `block_bits` on one device may be relied on, other than what follows from the above.
Results may differ from a plain program's by a relative error of at most 0.008.
The roundings to bfloat16 on the way count: a program that leaves them out, or rounds other values in their place, can miss the bound.
Values may be sent and summed in bfloat16 or wider, within the bound.
No kernel may reach another device: no remote copies, remote signals or barrier semaphores. Data moves between devices by JAX's collectives and lax.ppermute only.
A program may use at most 128 MiB of HBM per device.

v0:
```python
import jax
import jax.numpy as jnp
from jax import lax
from jax.sharding import PartitionSpec as P

LB_DEV = 2


epsilon = 1e-05


def label_side(column_sums, centroids):
    embed32 = column_sums * lax.rsqrt(
        jnp.mean(column_sums * column_sums, axis=1, keepdims=True) + epsilon
    )
    label_embed = embed32.astype(jnp.bfloat16)
    all_rows = lax.all_gather(centroids, "label", axis=0, tiled=True)
    scores = jnp.einsum("rd,kd->rk", label_embed, all_rows, preferred_element_type=jnp.float32)
    row_peak = jnp.max(scores, axis=1, keepdims=True)
    lifted = jnp.exp(scores - row_peak)
    membership = (lifted / jnp.sum(lifted, axis=1, keepdims=True)).astype(jnp.bfloat16)
    mixed_rows = jnp.dot(membership, all_rows, preferred_element_type=jnp.float32)
    return (label_embed, membership, mixed_rows.astype(jnp.bfloat16))


def body(features, inst_ids, lab_ids, counts, block_bits, centroids):
    dest_count, slot_cap = inst_ids.shape
    block_size = block_bits.shape[-1]
    feat_width = features.shape[1]
    inst_blocks = features.reshape(-1, block_size, feat_width)
    gathered = inst_blocks[inst_ids]
    incidence = block_bits.astype(jnp.bfloat16)
    partials = jnp.einsum(
        "ncab,ncad->ncbd", incidence, gathered, preferred_element_type=jnp.float32
    ).astype(jnp.bfloat16)
    filled = jnp.arange(slot_cap)[None, :] < counts[:, None]
    tagged_ids = jnp.where(filled, lab_ids, -1)
    arrived, arrived_ids = (
        lax.all_to_all(partials, "label", split_axis=0, concat_axis=0, tiled=True),
        lax.all_to_all(tagged_ids, "label", split_axis=0, concat_axis=0, tiled=True),
    )
    share_rows = LB_DEV * block_size
    col_blocks = lax.axis_size("dp") * LB_DEV
    slot_total = dest_count * slot_cap
    flat_ids = arrived_ids.reshape(slot_total)
    selector = (flat_ids[None, :] == jnp.arange(col_blocks)[:, None]).astype(jnp.bfloat16)
    column_sums = jnp.dot(
        selector,
        arrived.reshape(slot_total, block_size * feat_width),
        preferred_element_type=jnp.float32,
    )
    column_total = lax.psum(column_sums, "dp")
    embed_all, member_all, column_mixed = label_side(
        column_total.reshape(col_blocks * block_size, feat_width), centroids
    )
    offset = lax.axis_index("dp") * share_rows
    label_embed = lax.dynamic_slice_in_dim(embed_all, offset, share_rows, 0)
    membership = lax.dynamic_slice_in_dim(member_all, offset, share_rows, 0)
    mixed_blocks = column_mixed.reshape(col_blocks, block_size, feat_width)
    picked = mixed_blocks[jnp.maximum(arrived_ids, 0)]
    picked = jnp.where((arrived_ids >= 0)[:, :, None, None], picked, jnp.zeros_like(picked))
    returned = lax.all_to_all(picked, "label", split_axis=0, concat_axis=0, tiled=True)
    contrib = jnp.einsum("ncab,ncbd->ncad", incidence, returned, preferred_element_type=jnp.float32)
    owner_map = (
        inst_ids.reshape(slot_total)[None, :] == jnp.arange(inst_blocks.shape[0])[:, None]
    ).astype(jnp.float32)
    raw_targets = jnp.dot(
        owner_map,
        contrib.reshape(slot_total, block_size * feat_width),
        precision=lax.Precision.HIGHEST,
    )
    raw_targets = raw_targets.reshape(-1, feat_width)
    targets = raw_targets * lax.rsqrt(
        jnp.mean(raw_targets * raw_targets, axis=1, keepdims=True) + epsilon
    )
    return (label_embed, membership, targets.astype(jnp.bfloat16))


def solution(mesh):
    in_specs = (
        P(("dp", "label"), None),
        P(("dp", "label"), None),
        P(("dp", "label"), None),
        P(("dp", "label")),
        P(("dp", "label"), None, None, None),
        P("label", None),
    )
    out_specs = (P(("dp", "label"), None), P(("dp", "label"), None), P(("dp", "label"), None))
    return jax.shard_map(body, mesh=mesh, in_specs=in_specs, out_specs=out_specs, check_vma=False)
```

profile of v0, /device:TPU:61, one launch (start us, length us, event | category | flops | bytes accessed | tf_op | source)
XLA Modules:
  0.0 778.6 jit_solution(7269517425034337055)
XLA Ops:
  9.5 6.6 all-to-all-start
  17.0 7.3 gather_fusion
  24.3 10.8 %convert_bitcast_fusion = bf16[16,4,128,768]{2,3,1,0:T(8,128)(2,1)} fusion(bf16[16,4,128,768]{3,2,1,0:T(8,128)(2,1)} %bitcast.31, s32[16,4,128,128]{3,2,1,0:T(8,128)} %param.10), kind=kOutput, calls=%fused_computation.5 | convolution fusion | flops 1617952768 | bytes 29360128 | tf_op jit(solution)/shard_map/ncab,ncad->ncbd/dot_general | solution.py:33
  35.0 6.7 all-to-all-start.1
  43.0 219.8 %all-to-all-done.1 = bf16[16,4,128,768]{2,3,1,0:T(8,128)(2,1)} async-done(((bf16[16,4,128,768]{2,3,1,0:T(8,128)(2,1)}), bf16[16,4,128,768]{2,3,1,0:T(8,128)(2,1)}, u32[]{:S(2)}, u32[]{:S(2)}) %all-to-all-start.1) | async-done | bytes 12582944 | tf_op jit(solution)/shard_map/all_to_all | solution.py:39
  262.8 16.7 %copy.37 = bf16[8,8,128,768]{3,1,2,0:T(8,128)(2,1)} copy(bf16[8,8,128,768]{2,3,1,0:T(8,128)(2,1)} %bitcast.18) | data formatting | bytes 25165824
  279.5 9.0 %fusion.3 = f32[16,98304]{1,0:T(8,128)} fusion(bf16[64,98304]{1,0:T(8,128)(2,1)} %bitcast.34, s32[64]{0:T(128)S(1)} %eq.30), kind=kOutput, calls=%fused_computation.20 | convolution fusion | flops 201327616 | bytes 18874624 | tf_op jit(solution)/shard_map/dot_general | solution.py:47
  288.5 5.0 reshape.69
  294.4 91.7 %all-reduce.2.cloned.1.call-done = f32[2048,768]{1,0:T(8,128)} async-done(((f32[2048,768]{1,0:T(8,128)}), f32[2048,768]{1,0:T(8,128)}) %all-reduce.2.cloned.1.call-update) | async-done | bytes 6291472 | tf_op jit(solution)/shard_map/psum | solution.py:52
  386.2 3.4 multiply_reduce_fusion.1
  391.2 13.1 %fusion.7 = (f32[2048]{0:T(1024)S(1)}, f32[2048,2048]{0,1:T(8,128)}) fusion(bf16[2048,768]{1,0:T(8,128)(2,1)S(1)} %multiply_convert_fusion.1, bf16[2048,768]{1,0:T(8,128)(2,1)} %all-gather.2.cloned.1.call-done), kind=kOutput, calls=%fused_computation.32 | convolution fusion | flops 6446643200 | bytes 23076864 | tf_op jit(solution)/shard_map/rd,kd->rk/dot_general | solution.py:18
  404.4 8.1 %fusion = f32[2048]{0:T(1024)S(1)} fusion(f32[2048,2048]{0,1:T(8,128)} %get-tuple-element.15, f32[2048]{0:T(1024)S(1)} %get-tuple-element.14), kind=kLoop, calls=%fused_computation.4 | loop fusion | flops 8386560 | bytes 16793600 | tf_op jit(solution)/shard_map/reduce_sum | solution.py:21
  412.4 7.5 divide_convert_fusion
  419.9 7.3 convolution_convert_fusion
  427.3 7.2 gather_fusion.1
  434.4 16.6 %copy.34 = bf16[64,128,768]{1,2,0:T(8,128)(2,1)} copy(bf16[64,128,768]{2,1,0:T(8,128)(2,1)} %gather_fusion.1) | data formatting | bytes 25165824 | tf_op jit(solution)/shard_map/gather | solution.py:60
  451.1 10.6 %broadcast_select_fusion = bf16[16,4,128,768]{2,3,1,0:T(8,128)(2,1)} fusion(bf16[16,4,128,768]{2,3,1,0:T(8,128)(2,1)} %bitcast.32, pred[16,4]{1,0:T(8,128)(4,1)S(1)} %copy.33), kind=kLoop, calls=%fused_computation.6 | loop fusion | flops 6291456 | bytes 25165888 | tf_op jit(solution)/shard_map/jit(_where)/select_n | solution.py:61
  461.7 6.8 all-to-all-start.2
  473.2 232.6 %all-to-all-done.2 = bf16[16,4,128,768]{2,3,1,0:T(8,128)(2,1)} async-done(((bf16[16,4,128,768]{2,3,1,0:T(8,128)(2,1)}), bf16[16,4,128,768]{2,3,1,0:T(8,128)(2,1)}, u32[]{:S(2)}, u32[]{:S(2)}) %all-to-all-start.2) | async-done | bytes 12582944 | tf_op jit(solution)/shard_map/all_to_all | solution.py:62
  705.8 14.1 %convolution_bitcast_fusion = f32[16,4,128,768]{2,3,1,0:T(8,128)} fusion(bf16[16,4,128,768]{2,3,1,0:T(8,128)(2,1)} %all-to-all-done.2, s32[16,4,128,128]{3,2,1,0:T(8,128)} %param.10), kind=kOutput, calls=%fused_computation.7 | convolution fusion | flops 1611661312 | bytes 41943040 | tf_op jit(solution)/shard_map/ncab,ncbd->ncad/dot_general | solution.py:63
  719.9 25.1 %copy.38 = f32[8,8,128,768]{3,1,2,0:T(8,128)} copy(f32[8,8,128,768]{2,3,1,0:T(8,128)} %bitcast.29) | data formatting | bytes 50331648
  745.0 14.3 %fusion.4 = f32[16,98304]{1,0:T(8,128)} fusion(f32[64,98304]{1,0:T(8,128)} %bitcast.30, s32[64]{0:T(128)S(1)} %eq.34), kind=kOutput, calls=%fused_computation.21 | convolution fusion | flops 1207960576 | bytes 31457536 | tf_op jit(solution)/shard_map/dot_general | solution.py:67
  759.3 5.2 reshape.72
  764.5 3.4 multiply_reduce_fusion
  (45 shorter events, 14.1 us)
Async XLA Ops:
  8.0 9.0 %copy-start = (bf16[2048,768]{1,0:T(8,128)(2,1)S(1)}, bf16[2048,768]{1,0:T(8,128)(2,1)}, u32[]{:S(2)}) copy-start(bf16[2048,768]{1,0:T(8,128)(2,1)} %param.6) | copy-start | bytes 9437188
  9.5 25.5 %all-to-all-start = ((s32[16,1,4]{2,1,0:T(1,128)}), s32[16,1,4]{2,1,0:T(1,128)S(1)}, u32[]{:S(2)}, u32[]{:S(2)}) async-start(s32[16,1,4]{2,1,0:T(1,128)} %copy.27), calls=%async_computation | async-start | bytes 16384 | tf_op jit(solution)/shard_map/all_to_all | solution.py:40
  35.0 227.8 %all-to-all-start.1 = ((bf16[16,4,128,768]{2,3,1,0:T(8,128)(2,1)}), bf16[16,4,128,768]{2,3,1,0:T(8,128)(2,1)}, u32[]{:S(2)}, u32[]{:S(2)}) async-start(bf16[16,4,128,768]{2,3,1,0:T(8,128)(2,1)} %convert_bitcast_fusion), calls=%async_computation.1 | async-start | bytes 25165824 | tf_op jit(solution)/shard_map/all_to_all | solution.py:39
  41.7 344.5 %all-reduce.2.cloned.1.call-start = ((), (), s32[]{:S(2)}) async-start(), calls=%async_computation.3 | async-start | bytes 12582912 | tf_op jit(solution)/shard_map/psum | solution.py:52
  293.5 97.7 %all-gather.2.cloned.1.call-start = ((), (), s32[]{:S(2)}) async-start(), calls=%async_computation.4 | async-start | bytes 3342336 | tf_op jit(solution)/shard_map/all_gather | solution.py:17
  386.2 4.6 copy-start.3
  391.2 13.2 %copy-start.5 = (bf16[2048,768]{1,0:T(8,128)(2,1)}, bf16[2048,768]{1,0:T(8,128)(2,1)S(1)}, u32[]{:S(2)}) copy-start(bf16[2048,768]{1,0:T(8,128)(2,1)S(1)} %multiply_convert_fusion.1) | copy-start | bytes 9437188
  412.4 7.5 copy-start.7
  419.9 7.3 copy-start.4
  461.7 6.8 copy-start.6
  461.7 244.1 %all-to-all-start.2 = ((bf16[16,4,128,768]{2,3,1,0:T(8,128)(2,1)}), bf16[16,4,128,768]{2,3,1,0:T(8,128)(2,1)}, u32[]{:S(2)}, u32[]{:S(2)}) async-start(bf16[16,4,128,768]{2,3,1,0:T(8,128)(2,1)} %broadcast_select_fusion), calls=%async_computation.2 | async-start | bytes 25165824 | tf_op jit(solution)/shard_map/all_to_all | solution.py:62
  759.3 11.8 %copy-start.1 = (bf16[2048,768]{1,0:T(8,128)(2,1)S(1)}, bf16[2048,768]{1,0:T(8,128)(2,1)}, u32[]{:S(2)}) copy-start(bf16[2048,768]{1,0:T(8,128)(2,1)} %param.6) | copy-start | bytes 9437188
  764.5 4.6 copy-start.2
Sparse Core Ops, SparseCore 0:
  293.7 92.4 all-reduce.1
Sparse Core Ops, SparseCore 1:
  296.2 53.0 all-gather.1
where the time goes:
time: 780 us; the launch traced here: 779 us
  waiting for transfers between devices  545 us (70%)
  local copies, waits for them, and re-layouts  91.8 us (12%)
  matrix products  68.7 us (9%)
  other arithmetic  37.7 us (5%)
  starting transfers between devices  20.1 us (3%)
  between operations  15.6 us (2%)
    all_to_all x1, waiting for transfers between devices, body(): lax.all_to_all(picked, 'label', split_axis=0, concat_axis=0, tiled=True)  233 us
    all_to_all x1, waiting for transfers between devices, body(): lax.all_to_all(partials, 'label', split_axis=0, concat_axis=0, tiled=True)  220 us
    psum x1, waiting for transfers between devices, body(): column_total = lax.psum(column_sums, 'dp')  91.7 us
    unnamed x20, local copies, waits for them, and re-layouts  45.7 us
    gather x2, local copies, waits for them, and re-layouts, body(): picked = mixed_blocks[jnp.maximum(arrived_ids, 0)]  23.8 us
  transfers between devices with their start and end apart: 5, of which 3 were waited for; matrix products, arithmetic and copies ran while one was open for 4% of the time, Pallas kernels for 0%

commit v1 on v0

v1 whole, which is shorter than its diff:
```python
import functools

import jax
import jax.numpy as jnp
from jax import lax
from jax.experimental import pallas as pl
from jax.experimental.pallas import tpu as pltpu
from jax.sharding import PartitionSpec as P

LB_DEV = 2
EPSILON = 1e-05
CHUNKS = 1


def partial_kernel(cap, inst_ref, count_ref, bits_ref, feat_ref, out_ref):
    column = pl.program_id(0)
    block = bits_ref.shape[-1]
    for k in range(cap):

        @pl.when(k < count_ref[column])
        def _():
            incidence = bits_ref[0, k].astype(jnp.float32).astype(jnp.bfloat16)
            rows = feat_ref[inst_ref[column * cap + k]]
            part = lax.dot_general(
                incidence, rows, (((0,), (0,)), ((), ())), preferred_element_type=jnp.float32
            )
            out_ref[0, k * block : (k + 1) * block] = part.astype(jnp.bfloat16)


def partial_blocks(inst_flat, counts, block_bits, inst_blocks, chunk, width):
    columns, cap, block, _ = block_bits.shape
    n_inst = inst_blocks.shape[0]
    return pl.pallas_call(
        functools.partial(partial_kernel, cap),
        out_shape=jax.ShapeDtypeStruct((columns, cap * block, width), jnp.bfloat16),
        grid_spec=pltpu.PrefetchScalarGridSpec(
            num_scalar_prefetch=2,
            grid=(columns,),
            in_specs=[
                pl.BlockSpec((1, cap, block, block), lambda c, i, n: (c, 0, 0, 0)),
                pl.BlockSpec((n_inst, block, width), lambda c, i, n: (0, 0, chunk)),
            ],
            out_specs=pl.BlockSpec((1, cap * block, width), lambda c, i, n: (c, 0, 0)),
        ),
        name="partial_blocks",
    )(inst_flat, counts, block_bits, inst_blocks)


def sum_kernel(cap, ids_ref, arrived_ref, out_ref):
    sender = pl.program_id(0)
    block = out_ref.shape[1]

    @pl.when(sender == 0)
    def _():
        out_ref[...] = jnp.zeros_like(out_ref)

    for k in range(cap):
        target = ids_ref[sender * cap + k]

        @pl.when(target >= 0)
        def _():
            out_ref[target] += arrived_ref[0, k * block : (k + 1) * block].astype(jnp.float32)


def sum_blocks(flat_ids, arrived, col_blocks, block):
    senders, rows, width = arrived.shape
    cap = rows // block
    return pl.pallas_call(
        functools.partial(sum_kernel, cap),
        out_shape=jax.ShapeDtypeStruct((col_blocks, block, width), jnp.float32),
        grid_spec=pltpu.PrefetchScalarGridSpec(
            num_scalar_prefetch=1,
            grid=(senders,),
            in_specs=[pl.BlockSpec((1, rows, width), lambda e, ids: (e, 0, 0))],
            out_specs=pl.BlockSpec((col_blocks, block, width), lambda e, ids: (0, 0, 0)),
        ),
        name="sum_blocks",
    )(flat_ids, arrived)


def label_kernel(pieces, *refs):
    sum_refs, (cent_ref, embed_ref, member_ref, mixed_ref) = refs[:pieces], refs[pieces:]
    sums = [ref[...] for ref in sum_refs]
    sums = sums[0] if pieces == 1 else jnp.concatenate(sums, axis=1)
    embed = (sums * lax.rsqrt(jnp.mean(sums * sums, axis=1, keepdims=True) + EPSILON)).astype(jnp.bfloat16)
    embed_ref[...] = embed
    scores = lax.dot_general(embed, cent_ref[...], (((1,), (1,)), ((), ())), preferred_element_type=jnp.float32)
    lifted = jnp.exp(scores - jnp.max(scores, axis=1, keepdims=True))
    member = (lifted / jnp.sum(lifted, axis=1, keepdims=True)).astype(jnp.bfloat16)
    member_ref[...] = member
    mixed_ref[...] = jnp.dot(member, cent_ref[...], preferred_element_type=jnp.float32).astype(jnp.bfloat16)


def label_side(sums, centroids):
    rows = sums[0].shape[0]
    clusters, feat = centroids.shape
    tile = 128
    by_row = lambda i: (i, 0)
    return pl.pallas_call(
        functools.partial(label_kernel, len(sums)),
        out_shape=(
            jax.ShapeDtypeStruct((rows, feat), jnp.bfloat16),
            jax.ShapeDtypeStruct((rows, clusters), jnp.bfloat16),
            jax.ShapeDtypeStruct((rows, feat), jnp.bfloat16),
        ),
        grid=(rows // tile,),
        in_specs=[pl.BlockSpec((tile, s.shape[1]), by_row) for s in sums]
        + [pl.BlockSpec((clusters, feat), lambda i: (0, 0))],
        out_specs=(
            pl.BlockSpec((tile, feat), by_row),
            pl.BlockSpec((tile, clusters), by_row),
            pl.BlockSpec((tile, feat), by_row),
        ),
        name="label_side",
    )(*sums, centroids)


def target_kernel(cap, inst_ref, lab_ref, count_ref, bits_ref, *refs):
    mixed_refs, (out_ref, total) = refs[:cap], refs[cap:]
    column = pl.program_id(0)

    @pl.when(column == 0)
    def _():
        total[...] = jnp.zeros_like(total)

    for k in range(cap):

        @pl.when(k < count_ref[column])
        def _():
            incidence = bits_ref[0, k].astype(jnp.float32).astype(jnp.bfloat16)
            part = jnp.dot(incidence, mixed_refs[k][0], preferred_element_type=jnp.float32)
            total[inst_ref[column * cap + k]] += part

    @pl.when(column == pl.num_programs(0) - 1)
    def _():
        for g in range(total.shape[0]):
            raw = total[g]
            scale = lax.rsqrt(jnp.mean(raw * raw, axis=1, keepdims=True) + EPSILON)
            out_ref[g] = (raw * scale).astype(jnp.bfloat16)


def target_blocks(inst_flat, lab_flat, counts, block_bits, mixed_blocks, n_inst):
    columns, cap, block, _ = block_bits.shape
    feat = mixed_blocks.shape[-1]
    picked = [
        pl.BlockSpec((1, block, feat), lambda c, i, h, n, k=k: (h[c * cap + k], 0, 0)) for k in range(cap)
    ]
    return pl.pallas_call(
        functools.partial(target_kernel, cap),
        out_shape=jax.ShapeDtypeStruct((n_inst, block, feat), jnp.bfloat16),
        grid_spec=pltpu.PrefetchScalarGridSpec(
            num_scalar_prefetch=3,
            grid=(columns,),
            in_specs=[pl.BlockSpec((1, cap, block, block), lambda c, i, h, n: (c, 0, 0, 0))] + picked,
            out_specs=pl.BlockSpec((n_inst, block, feat), lambda c, i, h, n: (0, 0, 0)),
            scratch_shapes=[pltpu.VMEM((n_inst, block, feat), jnp.float32)],
        ),
        name="target_blocks",
    )(inst_flat, lab_flat, counts, block_bits, *([mixed_blocks] * cap))


def body(features, inst_ids, lab_ids, counts, block_bits, centroids):
    columns, cap = inst_ids.shape
    block = block_bits.shape[-1]
    feat = features.shape[1]
    inst_blocks = features.reshape(-1, block, feat)
    inst_flat = inst_ids.reshape(-1)
    filled = jnp.arange(cap)[None, :] < counts[:, None]
    tagged_ids = jnp.where(filled, lab_ids, -1)
    all_ids = lax.all_gather(tagged_ids, "label", axis=0, tiled=False)
    all_rows = lax.all_gather(centroids, "label", axis=0, tiled=True)
    arrived_ids = lax.dynamic_index_in_dim(all_ids, lax.axis_index("label"), axis=1, keepdims=False)
    flat_ids = arrived_ids.reshape(-1)
    col_blocks = lax.axis_size("dp") * LB_DEV

    width = feat // CHUNKS
    sums = []
    for chunk in range(CHUNKS):
        partials = partial_blocks(inst_flat, counts, block_bits, inst_blocks, chunk, width)
        arrived = lax.all_to_all(partials, "label", split_axis=0, concat_axis=0, tiled=True)
        column_sums = sum_blocks(flat_ids, arrived, col_blocks, block)
        sums.append(
            lax.psum_scatter(
                column_sums.reshape(col_blocks * block, width), "dp", scatter_dimension=0, tiled=True
            )
        )
    label_embed, membership, mixed = label_side(sums, all_rows)
    mixed_all = lax.all_gather(mixed, ("dp", "label"), axis=0, tiled=True)
    column = jnp.arange(columns, dtype=jnp.int32)[:, None]
    global_ids = (lab_ids // LB_DEV * columns + column) * LB_DEV + lab_ids % LB_DEV
    targets = target_blocks(
        inst_flat, global_ids.reshape(-1), counts, block_bits, mixed_all.reshape(-1, block, feat), inst_blocks.shape[0]
    )
    return (label_embed, membership, targets.reshape(features.shape))


def solution(mesh):
    in_specs = (
        P(("dp", "label"), None),
        P(("dp", "label"), None),
        P(("dp", "label"), None),
        P(("dp", "label")),
        P(("dp", "label"), None, None, None),
        P("label", None),
    )
    out_specs = (P(("dp", "label"), None), P(("dp", "label"), None), P(("dp", "label"), None))
    return jax.shard_map(body, mesh=mesh, in_specs=in_specs, out_specs=out_specs, check_vma=False)
```

time: 780 us -> 509 us (0.65)
  waiting for transfers between devices: 545 us -> 182 us
  blocking collectives: 0 us -> 240 us
  local copies, waits for them, and re-layouts: 91.8 us -> 3.07 us
  matrix products: 68.7 us -> 0 us
  Pallas kernels: 0 us -> 56.7 us
  other arithmetic: 37.7 us -> 0.02 us
  starting transfers between devices: 20.1 us -> 8.61 us
    all_gather x0 -> x1, blocking collectives: none -> 240 us  [body(): all_ids = lax.all_gather(tagged_ids, 'label', axis=0, tiled=False)]
    all_to_all x2 -> x0, waiting for transfers between devices: 233 us -> none  [the longest x1 233 us: body(): lax.all_to_all(picked, 'label', split_axis=0, concat_axis=0, tiled=True)]
    all_to_all x1, waiting for transfers between devices: 220 us -> 0.01 us  [body(): lax.all_to_all(partials, 'label', split_axis=0, concat_axis=0, tiled=True)]
    all_gather x1 -> x2, waiting for transfers between devices: 0.03 us -> 134 us  [the longest x1 134 us: body(): mixed_all = lax.all_gather(mixed, ('dp', 'label'), axis=0, tiled=True)]
    psum x1 -> x0, waiting for transfers between devices: 91.7 us -> none  [body(): column_total = lax.psum(column_sums, 'dp')]
    dot_general x6 -> x0, matrix products: 68.7 us -> none  [the longest x1 14.3 us: body(): jnp.dot(owner_map, contrib.reshape(slot_total, block_size * feat_width),...]
    pallas_call x0 -> x4, Pallas kernels: none -> 56.7 us  [the longest x1 18.1 us: target_blocks(): pl.pallas_call(functools.partial(target_kernel, cap), out_shape=jax.Shape...]
    reduce_scatter x0 -> x1, waiting for transfers between devices: none -> 47.7 us  [body(): lax.psum_scatter(column_sums.reshape(col_blocks * block, width), 'dp', sc...]
  transfers between devices with their start and end apart: 5 -> 4, of which waited for: 3 -> 2; matrix products, arithmetic and copies ran while one was open for 4% -> 0% of each run, Pallas kernels for 0% -> 3%
where the time goes in v1:
time: 509 us; the launch traced here: 507 us
  blocking collectives  240 us (47%)
  waiting for transfers between devices  182 us (36%)
  Pallas kernels  56.7 us (11%)
  between operations  15.5 us (3%)
  starting transfers between devices  8.61 us (2%)
    all_gather x1, blocking collectives, body(): all_ids = lax.all_gather(tagged_ids, 'label', axis=0, tiled=False)  240 us
    all_gather x1, waiting for transfers between devices, body(): mixed_all = lax.all_gather(mixed, ('dp', 'label'), axis=0, tiled=True)  134 us
    reduce_scatter x1, waiting for transfers between devices, body(): lax.psum_scatter(column_sums.reshape(col_blocks * block, width), 'dp', sc...  47.7 us
    pallas_call x1, Pallas kernels, target_blocks(): pl.pallas_call(functools.partial(target_kernel, cap), out_shape=jax.Shape...  18.1 us
    pallas_call x1, Pallas kernels, partial_blocks(): pl.pallas_call(functools.partial(partial_kernel, cap), out_shape=jax.Shap...  17.2 us
    pallas_call x1, Pallas kernels, sum_blocks(): pl.pallas_call(functools.partial(sum_kernel, cap), out_shape=jax.ShapeDty...  14.2 us
  transfers between devices with their start and end apart: 4, of which 2 were waited for; matrix products, arithmetic and copies ran while one was open for 0% of the time, Pallas kernels for 3%

profile of v1, /device:TPU:61, one launch (start us, length us, event | category | flops | bytes accessed | tf_op | source)
XLA Modules:
  0.0 506.6 jit_solution(1761401715490303975)
XLA Ops:
  8.0 0.8 copy.13
  8.8 0.6 reshape.30.inst_ref
  9.4 17.2 %partial_blocks.1 = bf16[16,512,768]{2,1,0:T(8,128)(2,1)} custom-call(s32[64]{0:T(128)} %reshape.30.inst_ref, s32[16]{0:T(128)} %count_ref.3, s32[16,4,128,128]{3,2,1,0:T(8,128)} %bits_ref.3, bf16[16,128,768]{2,1,0:T(8,128)(2,1)} %bitcast.11), custom_call_target="tpu_custom_call" | custom-call | tf_op jit(solution)/shard_map/partial_blocks/pallas_call | solution.py:33
  26.6 8.5 %all-to-all-start = ((bf16[16,512,768]{2,1,0:T(8,128)(2,1)}), bf16[16,512,768]{2,1,0:T(8,128)(2,1)}, u32[]{:S(2)}, u32[]{:S(2)}) async-start(bf16[16,512,768]{2,1,0:T(8,128)(2,1)} %partial_blocks.1), calls=%async_computation | async-start | bytes 25165824 | tf_op jit(solution)/shard_map/all_to_all | solution.py:180
  35.1 0.0 all-gather.5.cloned.1.call-start
  35.1 0.7 all-gather.5.cloned.1.call-update
  35.8 0.0 reduce-scatter.2.cloned.1.call-start
  35.9 0.0 copy-done
  35.9 0.0 copy-done.1
  35.9 240.4 %all-gather.1 = s32[16,16,4]{1,2,0:T(4,128)S(1)} all-gather(s32[1,16,4]{1,2,0:T(4,128)S(1)} %get-tuple-element.10), channel_id=2, replica_groups=mesh['dp'=8,'label'=16] {'label'}, dimensions={0}, use_global_device_ids=true | all-gather | bytes 4352 | tf_op jit(solution)/shard_map/all_gather | solution.py:170
  276.3 0.4 dynamic-slice_reduce_fusion
  276.7 0.6 reshape.29.ids_ref
  277.3 0.0 all-to-all-done.arrived_ref
  277.3 14.2 %sum_blocks.1 = f32[16,128,768]{2,1,0:T(8,128)} custom-call(s32[64]{0:T(128)} %reshape.29.ids_ref, bf16[16,512,768]{2,1,0:T(8,128)(2,1)} %all-to-all-done.arrived_ref), custom_call_target="tpu_custom_call" | custom-call | tf_op jit(solution)/shard_map/sum_blocks/pallas_call | solution.py:68
  291.5 0.0 reduce-scatter.2.cloned.1.call-update
  291.5 0.0 all-gather.7.cloned.1.call-start
  291.6 0.0 all-gather.5.cloned.1.call-done.refs_1_
  291.6 47.7 %reduce-scatter.2.cloned.1.call-done.refs_0_ = f32[256,768]{1,0:T(8,128)} async-done(((f32[2048,768]{1,0:T(8,128)}), f32[256,768]{1,0:T(8,128)}) %reduce-scatter.2.cloned.1.call-update) | async-done | bytes 786448 | tf_op jit(solution)/shard_map/reduce_scatter | solution.py:183
  339.3 7.2 %label_side.1 = (bf16[256,768]{1,0:T(8,128)(2,1)}, bf16[256,2048]{1,0:T(8,128)(2,1)}, bf16[256,768]{1,0:T(8,128)(2,1)}) custom-call(f32[256,768]{1,0:T(8,128)} %reduce-scatter.2.cloned.1.call-done.refs_0_, bf16[2048,768]{1,0:T(8,128)(2,1)} %all-gather.5.cloned.1.call-done.refs_1_), custom_call_target="tpu_custom_call" | custom-call | tf_op jit(solution)/shard_map/label_side/pallas_call | solution.py:99
  346.6 0.0 all-gather.7.cloned.1.call-update
  346.6 0.1 copy.14
  346.7 0.6 reshape.33.lab_ref
  347.2 133.8 %all-gather.7.cloned.1.call-done = bf16[32768,768]{1,0:T(8,128)(2,1)} async-done(((bf16[256,768]{1,0:T(8,128)(2,1)}), bf16[32768,768]{1,0:T(8,128)(2,1)}) %all-gather.7.cloned.1.call-update) | async-done | bytes 50331664 | tf_op jit(solution)/shard_map/all_gather | solution.py:188
  481.0 18.1 %target_blocks.1 = bf16[16,128,768]{2,1,0:T(8,128)(2,1)} custom-call(s32[64]{0:T(128)} %reshape.30.inst_ref, s32[64]{0:T(128)} %reshape.33.lab_ref, s32[16]{0:T(128)} %count_ref.3, s32[16,4,128,128]{3,2,1,0:T(8,128)} %bits_ref.3, bf16[256,128,768]{2,1,0:T(8,128)(2,1)} %bitcast.6, bf16[256,128,768]{2,1,0:T(8,128)(2,1)} %bitcast.7, ...), custom_call_target="tpu_custom_call" | custom-call | tf_op jit(solution)/shard_map/target_blocks/pallas_call | solution.py:148
  (3 shorter events, 0.0 us)
Async XLA Ops:
  26.6 9.3 %copy-start = (s32[16]{0:T(128)S(1)}, s32[16]{0:T(128)}, u32[]{:S(2)}) copy-start(s32[16]{0:T(128)} %count_ref.3) | copy-start | bytes 196
  26.6 9.3 %copy-start.1 = (s32[16,4]{0,1:T(4,128)S(1)}, s32[16,4]{0,1:T(4,128)}, u32[]{:S(2)}) copy-start(s32[16,4]{0,1:T(4,128)} %param.8) | copy-start | bytes 772
  26.6 250.7 %all-to-all-start = ((bf16[16,512,768]{2,1,0:T(8,128)(2,1)}), bf16[16,512,768]{2,1,0:T(8,128)(2,1)}, u32[]{:S(2)}, u32[]{:S(2)}) async-start(bf16[16,512,768]{2,1,0:T(8,128)(2,1)} %partial_blocks.1), calls=%async_computation | async-start | bytes 25165824 | tf_op jit(solution)/shard_map/all_to_all | solution.py:180
  35.1 256.5 %all-gather.5.cloned.1.call-start = ((), (), s32[]{:S(2)}) async-start(), calls=%async_computation.3 | async-start | bytes 3342336 | tf_op jit(solution)/shard_map/all_gather | solution.py:171
  35.8 303.5 %reduce-scatter.2.cloned.1.call-start = ((), (), s32[]{:S(2)}) async-start(), calls=%async_computation.2 | async-start | bytes 7077888 | tf_op jit(solution)/shard_map/reduce_scatter | solution.py:183
  291.5 189.5 %all-gather.7.cloned.1.call-start = ((), (), s32[]{:S(2)}) async-start(), calls=%async_computation.4 | async-start | bytes 50724864 | tf_op jit(solution)/shard_map/all_gather | solution.py:188
Sparse Core Ops, SparseCore 0:
  38.1 235.8 all-gather.4
  346.7 134.2 all-gather.6
Sparse Core Ops, SparseCore 1:
  291.6 47.7 reduce-scatter.1

commit v2 on v1

v2 whole, which is shorter than its diff:
```python
import functools

import jax
import jax.numpy as jnp
from jax import lax
from jax.experimental import pallas as pl
from jax.experimental.pallas import tpu as pltpu
from jax.sharding import PartitionSpec as P


LB_DEV = 2
EPSILON = 1e-05
SUM_STEPS = 2
LABEL_TILE = 256
TARGET_GROUP = 8
SIDE = 4
SPLITS = ((256, 0), (128, 4))


MAKE = (
    (0, ((0, 1),)),
    (0, ((1, 1),)),
    (0, ((0, 3), (0, 2))),
    (0, ((1, 3), (1, 2))),
    (1, ((0, 1), (0, 3), (0, 2))),
    (1, ((1, 1), (1, 3), (1, 2))),
    (0, ((0, 0), (1, 0))),
    (1, ((0, 0), (1, 0))),
)


def mod4(value):
    return jnp.bitwise_and(value, SIDE - 1)


def shift_first(array, step):
    pairs = [(a * SIDE + b, (a + step) % SIDE * SIDE + b) for a in range(SIDE) for b in range(SIDE)]
    return lax.ppermute(array, "label", pairs)


def shift_second(array, step):
    pairs = [(a * SIDE + b, a * SIDE + (b + step) % SIDE) for a in range(SIDE) for b in range(SIDE)]
    return lax.ppermute(array, "label", pairs)


def shift_plane(array, step):
    pairs = [(a * 2 + b, (a + step) % SIDE * 2 + b) for a in range(SIDE) for b in range(2)]
    return lax.ppermute(array, "dp", pairs)


def swap_core(array):
    return lax.ppermute(array, "dp", [(a * 2 + b, a * 2 + 1 - b) for a in range(SIDE) for b in range(2)])


def partial_kernel(cap, groups, axes, pos_ref, inst_ref, *refs):
    bits_refs, refs = refs[: len(groups)], refs[len(groups) :]
    feat_refs, out_refs = dict(zip(axes, refs)), refs[len(axes) :]
    for (first_axis, outer), bits_ref, out_ref in zip(groups, bits_refs, out_refs):
        fixed = mod4(pos_ref[first_axis] + outer)
        for inner in range(SIDE):
            other = mod4(pos_ref[1 - first_axis] + inner)
            column = fixed * SIDE + other if first_axis == 0 else other * SIDE + fixed
            for k in range(cap):
                incidence = bits_ref[0, other, k] if first_axis == 0 else bits_ref[other, 0, k]
                part = lax.dot_general(
                    incidence.astype(jnp.float32).astype(jnp.bfloat16),
                    feat_refs[first_axis][inst_ref[column * cap + k]],
                    (((0,), (0,)), ((), ())),
                    preferred_element_type=jnp.float32,
                )
                out_ref[inner, k] = part.astype(jnp.bfloat16)


def partial_blocks(pos, inst_flat, block_bits, inst_blocks, groups, part):
    _, cap, block, _ = block_bits.shape
    n_inst = inst_blocks.shape[0]
    width, start = SPLITS[part]
    grid_bits = block_bits.reshape(SIDE, SIDE, cap, block, block)
    axes = tuple(sorted({first_axis for first_axis, _ in groups}))
    bits_specs = []
    for first_axis, outer in groups:
        if first_axis == 0:
            shape, index = (1, SIDE), lambda g, p, i, outer=outer: (mod4(p[0] + outer), 0, 0, 0, 0)
        else:
            shape, index = (SIDE, 1), lambda g, p, i, outer=outer: (0, mod4(p[1] + outer), 0, 0, 0)
        bits_specs.append(pl.BlockSpec(shape + (cap, block, block), index))
    feat_specs = [
        pl.BlockSpec((n_inst, block, width), lambda g, p, i, at=start + axis: (0, 0, at)) for axis in axes
    ]
    out = jax.ShapeDtypeStruct((SIDE, cap, block, width), jnp.bfloat16)
    return pl.pallas_call(
        functools.partial(partial_kernel, cap, groups, axes),
        out_shape=(out,) * len(groups),
        grid_spec=pltpu.PrefetchScalarGridSpec(
            num_scalar_prefetch=2,
            grid=(1,),
            in_specs=bits_specs + feat_specs,
            out_specs=(pl.BlockSpec(out.shape, lambda g, p, i: (0, 0, 0, 0)),) * len(groups),
        ),
        cost_estimate=pl.CostEstimate(
            flops=2 * len(groups) * SIDE * cap * block * block * width,
            bytes_accessed=len(groups) * (4 << 20),
            transcendentals=0,
        ),
        name="partial_blocks",
    )(pos, inst_flat, *([grid_bits] * len(groups)), *([inst_blocks] * len(axes)))


def pack_kernel(*refs):
    ins, outs = refs[:SIDE], refs[SIDE:]
    for outer, out_ref in enumerate(outs, start=1):
        for step, ref in enumerate(ins):
            out_ref[step] = ref[outer]


def pack_groups(received):
    shape = received[0].shape
    whole = pl.BlockSpec(shape, lambda i: (0, 0, 0, 0))
    return pl.pallas_call(
        pack_kernel,
        out_shape=(jax.ShapeDtypeStruct(shape, received[0].dtype),) * (SIDE - 1),
        grid=(1,),
        in_specs=[whole] * len(received),
        out_specs=(whole,) * (SIDE - 1),
        cost_estimate=pl.CostEstimate(flops=0, bytes_accessed=8 << 20, transcendentals=0),
        name="pack_groups",
    )(*received)


def sum_kernel(cap, width, pos_ref, ids_ref, *refs):
    arrived, (keep_ref, send_ref, total) = refs[: 4 * SIDE - 2], refs[4 * SIDE - 2 :]
    half = keep_ref.shape[0]
    per_step = SIDE // SUM_STEPS
    at = pl.program_id(0) * per_step

    @pl.when(at == 0)
    def _():
        total[...] = jnp.zeros_like(total)

    def add(first_axis, outer, inner, ref, row_at):
        step = (inner, outer) if first_axis == 0 else (outer, inner)
        sender = step[0] * SIDE + step[1]
        for k in range(cap):
            target = ids_ref[sender * cap + k]

            @pl.when(target >= 0)
            def _():
                away = jnp.bitwise_xor(jnp.bitwise_and(target >> 1, 1), pos_ref[3])
                row = away * half + mod4((target >> 2) - pos_ref[2]) * LB_DEV + jnp.bitwise_and(target, 1)
                columns = pl.ds(first_axis * width, width)
                total[row, :, columns] += ref[row_at, k].astype(jnp.float32)

    for first_axis in range(2):
        refs_here = arrived[first_axis * (2 * SIDE - 1) : (first_axis + 1) * (2 * SIDE - 1)]
        for step in range(SIDE):

            @pl.when(at == step // per_step * per_step)
            def _():
                add(first_axis, 0, step, refs_here[step], 0)

        for outer in range(1, SIDE):
            for step in range(per_step):
                add(first_axis, outer, at + step, refs_here[SIDE - 1 + outer], step)

    @pl.when(at == SIDE - per_step)
    def _():
        keep_ref[...] = total[:half]
        send_ref[...] = total[half:]


def sum_blocks(pos, flat_ids, arrived, col_blocks):
    _, cap, block, width = arrived[0].shape
    half = jax.ShapeDtypeStruct((col_blocks // 2, block, 2 * width), jnp.float32)
    whole = pl.BlockSpec(half.shape, lambda j, p, i: (0, 0, 0))
    own = pl.BlockSpec((1, cap, block, width), lambda j, p, i: (0, 0, 0, 0))
    far = pl.BlockSpec((SIDE // SUM_STEPS, cap, block, width), lambda j, p, i: (j, 0, 0, 0))
    return pl.pallas_call(
        functools.partial(sum_kernel, cap, width),
        out_shape=(half, half),
        grid_spec=pltpu.PrefetchScalarGridSpec(
            num_scalar_prefetch=2,
            grid=(SUM_STEPS,),
            in_specs=([own] * SIDE + [far] * (SIDE - 1)) * 2,
            out_specs=(whole, whole),
            scratch_shapes=[pltpu.VMEM((col_blocks, block, 2 * width), jnp.float32)],
        ),
        cost_estimate=pl.CostEstimate(
            flops=SIDE * SIDE * cap * block * 2 * width, bytes_accessed=12 << 20, transcendentals=0
        ),
        name="sum_blocks",
    )(pos, flat_ids, *arrived)


def label_kernel(*refs):
    sum_refs, (cent_ref, embed_ref, member_ref, mixed_ref) = refs[:-4], refs[-4:]
    sums = []
    for at in range(0, len(sum_refs), SIDE):
        sums.append(sum_refs[at][...] + sum_refs[at + 1][...] + sum_refs[at + 2][...] + sum_refs[at + 3][...])
    sums = jnp.concatenate(sums, axis=1)
    embed = (sums * lax.rsqrt(jnp.mean(sums * sums, axis=1, keepdims=True) + EPSILON)).astype(jnp.bfloat16)
    embed_ref[...] = embed
    scores = lax.dot_general(embed, cent_ref[...], (((1,), (1,)), ((), ())), preferred_element_type=jnp.float32)
    lifted = jnp.exp(scores - jnp.max(scores, axis=1, keepdims=True))
    member = (lifted / jnp.sum(lifted, axis=1, keepdims=True)).astype(jnp.bfloat16)
    member_ref[...] = member
    mixed_ref[...] = jnp.dot(member, cent_ref[...], preferred_element_type=jnp.float32).astype(jnp.bfloat16)


def label_side(sums, centroids):
    rows = sums[0].shape[0]
    clusters, feat = centroids.shape
    tile = LABEL_TILE
    by_row = lambda i: (i, 0)
    return pl.pallas_call(
        label_kernel,
        out_shape=(
            jax.ShapeDtypeStruct((rows, feat), jnp.bfloat16),
            jax.ShapeDtypeStruct((rows, clusters), jnp.bfloat16),
            jax.ShapeDtypeStruct((rows, feat), jnp.bfloat16),
        ),
        grid=(rows // tile,),
        in_specs=[pl.BlockSpec((tile, s.shape[1]), by_row) for s in sums]
        + [pl.BlockSpec((clusters, feat), lambda i: (0, 0))],
        out_specs=(
            pl.BlockSpec((tile, feat), by_row),
            pl.BlockSpec((tile, clusters), by_row),
            pl.BlockSpec((tile, feat), by_row),
        ),
        name="label_side",
    )(*sums, centroids)


def target_kernel(group, count_ref, slot_ref, inst_ref, lab_ref, *refs):
    bits_refs, mixed_refs, (out_ref, total) = refs[:group], refs[group : 2 * group], refs[2 * group :]
    at = pl.program_id(0) * group

    @pl.when(at == 0)
    def _():
        total[...] = jnp.zeros_like(total)

    @pl.when(at < count_ref[0])
    def _():
        for k in range(group):
            used = (at + k < count_ref[0]).astype(jnp.int32)
            incidence = (bits_refs[k][0] * used).astype(jnp.float32).astype(jnp.bfloat16)
            part = jnp.dot(incidence, mixed_refs[k][0], preferred_element_type=jnp.float32)
            total[inst_ref[at + k]] += part

    @pl.when(at + group == group * pl.num_programs(0))
    def _():
        for g in range(total.shape[0]):
            raw = total[g]
            scale = lax.rsqrt(jnp.mean(raw * raw, axis=1, keepdims=True) + EPSILON)
            out_ref[g] = (raw * scale).astype(jnp.bfloat16)


def target_blocks(slots, insts, labs, n_used, block_bits, mixed_blocks, n_inst):
    n_slots, block, _ = block_bits.shape
    feat = mixed_blocks.shape[-1]
    group = TARGET_GROUP

    def pick(table, k):
        def index(g, n, *tables):
            return (tables[table][jnp.minimum(g, (jnp.maximum(n[0], 1) - 1) // group) * group + k], 0, 0)

        return index

    return pl.pallas_call(
        functools.partial(target_kernel, group),
        out_shape=jax.ShapeDtypeStruct((n_inst, block, feat), jnp.bfloat16),
        grid_spec=pltpu.PrefetchScalarGridSpec(
            num_scalar_prefetch=4,
            grid=(n_slots // group,),
            in_specs=[pl.BlockSpec((1, block, block), pick(0, k)) for k in range(group)]
            + [pl.BlockSpec((1, block, feat), pick(2, k)) for k in range(group)],
            out_specs=pl.BlockSpec((n_inst, block, feat), lambda g, *tables: (0, 0, 0)),
            scratch_shapes=[pltpu.VMEM((n_inst, block, feat), jnp.float32)],
        ),
        name="target_blocks",
    )(n_used, slots, insts, labs, *([block_bits] * group), *([mixed_blocks] * group))


def body(features, inst_ids, lab_ids, counts, block_bits, centroids):
    columns, cap = inst_ids.shape
    block = block_bits.shape[-1]
    feat = features.shape[1]
    planes = lax.axis_size("dp")
    inst_blocks = features.reshape(-1, block, feat)
    inst_flat = inst_ids.reshape(-1)
    d = lax.axis_index("dp")
    e = lax.axis_index("label")
    pos = jnp.stack([e // SIDE, e % SIDE, d // 2, d % 2]).astype(jnp.int32)

    filled = jnp.arange(cap)[None, :] < counts[:, None]
    tagged_ids = jnp.where(filled, lab_ids, -1).reshape(SIDE, SIDE, cap)
    tagged_ids = jnp.roll(tagged_ids, (-(e // SIDE), -(e % SIDE)), (0, 1))
    near = [shift_first(tagged_ids[step], step) if step else tagged_ids[0] for step in range(SIDE)]
    near = jnp.stack(near, axis=1)
    near = [shift_second(near[step], step) if step else near[0] for step in range(SIDE)]
    flat_ids = jnp.stack(near, axis=1).reshape(-1)

    share = centroids.shape[0] // planes
    own_rows = lax.dynamic_slice_in_dim(centroids, d * share, share, 0)
    all_rows = lax.all_gather(own_rows, ("label", "dp"), axis=0, tiled=True)

    shifts = (shift_first, shift_second)
    sums = []
    stage = {}
    for part, groups in MAKE:
        made = partial_blocks(pos, inst_flat, block_bits, inst_blocks, groups, part)
        for (first_axis, outer), blocks in zip(groups, made):
            stage[part, first_axis, outer] = shifts[first_axis](blocks, outer) if outer else blocks
    for part in range(len(SPLITS)):
        arrived = []
        for first_axis in range(2):
            received = [stage[part, first_axis, step] for step in range(SIDE)]
            arrived += received
            packed = pack_groups(received)
            for outer, group in enumerate(packed, start=1):
                arrived.append(shifts[1 - first_axis](group, outer))
        keep, send = sum_blocks(pos, flat_ids, arrived, planes * LB_DEV)
        other = swap_core(send)
        for step in range(SIDE):
            rows = slice(step * LB_DEV, (step + 1) * LB_DEV)
            piece = (keep[rows] + other[rows]).reshape(LB_DEV * block, -1)
            sums.append(shift_plane(piece, step) if step else piece)
    label_embed, membership, mixed = label_side(sums, all_rows)
    mixed_all = lax.all_gather(mixed, ("dp", "label"), axis=0, tiled=True)

    column = jnp.arange(columns, dtype=jnp.int32)[:, None]
    global_ids = ((lab_ids // LB_DEV * columns + column) * LB_DEV + lab_ids % LB_DEV).reshape(-1)
    used = filled.reshape(-1)
    place = jnp.where(used, jnp.cumsum(used) - 1, used.size)
    slots = jnp.arange(used.size, dtype=jnp.int32)
    chosen = (place[None, :] == slots[:, None]).astype(jnp.int32)
    tables = [jnp.sum(chosen * table[None, :], axis=1) for table in (slots, inst_flat, global_ids)]
    n_used = jnp.sum(used, dtype=jnp.int32).reshape(1)
    targets = target_blocks(
        *tables, n_used, block_bits.reshape(-1, block, block), mixed_all.reshape(-1, block, feat), inst_blocks.shape[0]
    )
    return (label_embed, membership, targets.reshape(features.shape))


def solution(mesh):
    in_specs = (
        P(("dp", "label"), None),
        P(("dp", "label"), None),
        P(("dp", "label"), None),
        P(("dp", "label")),
        P(("dp", "label"), None, None, None),
        P("label", None),
    )
    out_specs = (P(("dp", "label"), None), P(("dp", "label"), None), P(("dp", "label"), None))
    return jax.shard_map(body, mesh=mesh, in_specs=in_specs, out_specs=out_specs, check_vma=False)
```

time: 509 us -> 451 us (0.89)
  blocking collectives: 240 us -> 0 us
  waiting for transfers between devices: 182 us -> 272 us
  starting transfers between devices: 8.61 us -> 69.8 us
  Pallas kernels: 56.7 us -> 79.7 us
  other arithmetic: 0.02 us -> 5.66 us
    all_gather x1 -> x0, blocking collectives: 240 us -> none  [body(): all_ids = lax.all_gather(tagged_ids, 'label', axis=0, tiled=False)]
    ppermute x0 -> x38, waiting for transfers between devices: none -> 140 us  [the longest x15 62 us: shift_second(): return lax.ppermute(array, 'label', pairs)]
    ppermute x0 -> x38, starting transfers between devices: none -> 69.7 us  [the longest x15 26.7 us: shift_first(): return lax.ppermute(array, 'label', pairs)]
    reduce_scatter x1 -> x0, waiting for transfers between devices: 47.7 us -> none  [body(): lax.psum_scatter(column_sums.reshape(col_blocks * block, width), 'dp', sc...]
    pallas_call x4 -> x16, Pallas kernels: 56.7 us -> 79.7 us  [the longest x8 33.4 us: partial_blocks(): pl.pallas_call(functools.partial(partial_kernel, cap, groups, axes), out_...]
    all_to_all x1 -> x0, starting transfers between devices: 8.49 us -> none  [body(): lax.all_to_all(partials, 'label', split_axis=0, concat_axis=0, tiled=True)]
  transfers between devices with their start and end apart: 4 -> 40, of which waited for: 2 -> 20; matrix products, arithmetic and copies ran while one was open for 0% -> 2% of each run, Pallas kernels for 3% -> 13%
where the time goes in v2:
time: 451 us; the launch traced here: 447 us
  waiting for transfers between devices  272 us (60%)
  Pallas kernels  79.7 us (18%)
  starting transfers between devices  69.8 us (15%)
  between operations  14.4 us (3%)
  local copies, waits for them, and re-layouts  5.95 us (1%)
  other arithmetic  5.66 us (1%)
    all_gather x1, waiting for transfers between devices, body(): mixed_all = lax.all_gather(mixed, ('dp', 'label'), axis=0, tiled=True)  132 us
    ppermute x15, waiting for transfers between devices, shift_second(): return lax.ppermute(array, 'label', pairs)  62 us
    ppermute x15, waiting for transfers between devices, shift_first(): return lax.ppermute(array, 'label', pairs)  44.8 us
    pallas_call x8, Pallas kernels, partial_blocks(): pl.pallas_call(functools.partial(partial_kernel, cap, groups, axes), out_...  33.4 us
    ppermute x6, waiting for transfers between devices, shift_plane(): return lax.ppermute(array, 'dp', pairs)  30.4 us
    ppermute x15, starting transfers between devices, shift_first(): return lax.ppermute(array, 'label', pairs)  26.7 us
    ppermute x15, starting transfers between devices, shift_second(): return lax.ppermute(array, 'label', pairs)  23.1 us
    ppermute x2, starting transfers between devices, swap_core(): lax.ppermute(array, 'dp', [(a * 2 + b, a * 2 + 1 - b) for a in range(SIDE...  13.7 us
  transfers between devices with their start and end apart: 40, of which 20 were waited for; matrix products, arithmetic and copies ran while one was open for 2% of the time, Pallas kernels for 13%

profile of v2, /device:TPU:61, one launch (start us, length us, event | category | flops | bytes accessed | tf_op | source)
XLA Modules:
  0.0 447.2 jit_solution(12563469485985800213)
XLA Ops:
  13.9 4.4 partial_blocks.10
  24.0 4.5 partial_blocks.12
  31.3 4.7 %partial_blocks.8 = (bf16[4,4,128,256]{3,2,1,0:T(8,128)(2,1)}, bf16[4,4,128,256]{3,2,1,0:T(8,128)(2,1)}) custom-call(s32[4]{0:T(128)} %pad_add_fusion.2.pos_ref, s32[64]{0:T(128)} %reshape.131.inst_ref, s32[4,4,4,128,128]{4,3,2,1,0:T(8,128)} %bitcast.48, s32[4,4,4,128,128]{4,3,2,1,0:T(8,128)} %bitcast.49, bf16[16,128,768]{2,1,0:T(8,128)(2,1)} %bitcast.70, ...), custom_call_target="tpu_custom_call" | custom-call | flops 268435456 | bytes 8388608 | tf_op jit(solution)/shard_map/partial_blocks/pallas_call | solution.py:91
  38.0 22.0 %collective-permute-done.7.refs_2_ = bf16[4,4,128,256]{3,2,1,0:T(8,128)(2,1)S(1)} collective-permute-done((bf16[4,4,128,256]{3,2,1,0:T(8,128)(2,1)}, bf16[4,4,128,256]{3,2,1,0:T(8,128)(2,1)S(1)}, u32[]{:S(2)}, u32[]{:S(2)}) %collective-permute-start.7) | collective-permute-done | bytes 1048608 | tf_op jit(solution)/shard_map/ppermute | solution.py:38
  60.0 6.0 %collective-permute-done.8.refs_3_ = bf16[4,4,128,256]{3,2,1,0:T(8,128)(2,1)S(1)} collective-permute-done((bf16[4,4,128,256]{3,2,1,0:T(8,128)(2,1)}, bf16[4,4,128,256]{3,2,1,0:T(8,128)(2,1)S(1)}, u32[]{:S(2)}, u32[]{:S(2)}) %collective-permute-start.8) | collective-permute-done | bytes 1048608 | tf_op jit(solution)/shard_map/ppermute | solution.py:38
  89.6 7.9 %collective-permute-start.3 = (s32[4,4]{1,0:T(4,128)S(1)}, s32[4,4]{1,0:T(4,128)S(1)}, u32[]{:S(2)}, u32[]{:S(2)}) collective-permute-start(s32[4,4]{1,0:T(4,128)S(1)} %bitcast.94), channel_id=1, source_target_pairs={{0,1},{1,2},{2,3},{3,0},{4,5},{5,6},{6,7},{7,4},{8,9},{9,10},{10,1... | collective-permute-start | bytes 200 | tf_op jit(solution)/shard_map/ppermute | solution.py:43
  97.4 4.2 partial_blocks.15
  106.7 4.1 pack_groups.5
  110.8 5.4 %collective-permute-done.28.refs_1_.refs_8_ = bf16[4,4,128,128]{3,2,1,0:T(8,128)(2,1)S(1)} collective-permute-done((bf16[4,4,128,128]{3,2,1,0:T(8,128)(2,1)}, bf16[4,4,128,128]{3,2,1,0:T(8,128)(2,1)S(1)}, u32[]{:S(2)}, u32[]{:S(2)}) %collective-permute-start.28) | collective-permute-done | bytes 524320 | tf_op jit(solution)/shard_map/ppermute | solution.py:43
  120.7 12.3 %collective-permute-done.30.refs_3_.refs_10_ = bf16[4,4,128,128]{3,2,1,0:T(8,128)(2,1)S(1)} collective-permute-done((bf16[4,4,128,128]{3,2,1,0:T(8,128)(2,1)}, bf16[4,4,128,128]{3,2,1,0:T(8,128)(2,1)S(1)}, u32[]{:S(2)}, u32[]{:S(2)}) %collective-permute-start.30) | collective-permute-done | bytes 524320 | tf_op jit(solution)/shard_map/ppermute | solution.py:43
  136.4 4.3 partial_blocks.14
  140.7 10.8 %collective-permute-done.10.refs_5_ = bf16[4,4,128,256]{3,2,1,0:T(8,128)(2,1)} collective-permute-done((bf16[4,4,128,256]{3,2,1,0:T(8,128)(2,1)}, bf16[4,4,128,256]{3,2,1,0:T(8,128)(2,1)}, u32[]{:S(2)}, u32[]{:S(2)}) %collective-permute-start.10) | collective-permute-done | bytes 1048608 | tf_op jit(solution)/shard_map/ppermute | solution.py:43
  154.5 3.9 partial_blocks.13
  158.4 17.5 %collective-permute-done.11.refs_6_ = bf16[4,4,128,256]{3,2,1,0:T(8,128)(2,1)} collective-permute-done((bf16[4,4,128,256]{3,2,1,0:T(8,128)(2,1)}, bf16[4,4,128,256]{3,2,1,0:T(8,128)(2,1)}, u32[]{:S(2)}, u32[]{:S(2)}) %collective-permute-start.11) | collective-permute-done | bytes 1048608 | tf_op jit(solution)/shard_map/ppermute | solution.py:43
  184.5 7.9 %sum_blocks.2 = (f32[8,128,512]{2,1,0:T(8,128)}, f32[8,128,512]{2,1,0:T(8,128)}) custom-call(s32[4]{0:T(128)} %pad_add_fusion.2.pos_ref, s32[64]{0:T(128)} %reshape.130.ids_ref, bf16[4,4,128,256]{3,2,1,0:T(8,128)(2,1)} %get-tuple-element.36.refs_0_, bf16[4,4,128,256]{3,2,1,0:T(8,128)(2,1)} %copy-done.2, bf16[4,4,128,256]{3,2,1,0:T(8,128)(2,1)} %copy-done.3, ...), custom_call_target="tpu_custom_call" | custom-call | flops 4194304 | bytes 12582912 | tf_op jit(solution)/shard_map/sum_blocks/pallas_call | solution.py:177
  192.4 11.9 %collective-permute-start.18 = (f32[8,128,512]{2,1,0:T(8,128)}, f32[8,128,512]{2,1,0:T(8,128)S(1)}, u32[]{:S(2)}, u32[]{:S(2)}) collective-permute-start(f32[8,128,512]{2,1,0:T(8,128)} %get-tuple-element.49), channel_id=1, source_target_pairs={{0,16},{16,0},{32,48},{48,32},{64,80},{80,64},{96,112},{112,96},{1... | collective-permute-start | bytes 6291464 | tf_op jit(solution)/shard_map/ppermute | solution.py:52
  212.8 5.6 %collective-permute-start.27 = (bf16[4,4,128,128]{3,2,1,0:T(8,128)(2,1)}, bf16[4,4,128,128]{3,2,1,0:T(8,128)(2,1)}, u32[]{:S(2)}, u32[]{:S(2)}) collective-permute-start(bf16[4,4,128,128]{3,2,1,0:T(8,128)(2,1)} %get-tuple-element.56), channel_id=1, source_target_pairs={{0,3},{1,0},{2,1},{3,2},{4,7},{5,4},{6,5},{7,6},{8,11},{9,8},{10,9... | collective-permute-start | bytes 1572872 | tf_op jit(solution)/shard_map/ppermute | solution.py:43
  218.4 8.6 %collective-permute-done.33.refs_13_ = bf16[4,4,128,128]{3,2,1,0:T(8,128)(2,1)} collective-permute-done((bf16[4,4,128,128]{3,2,1,0:T(8,128)(2,1)}, bf16[4,4,128,128]{3,2,1,0:T(8,128)(2,1)}, u32[]{:S(2)}, u32[]{:S(2)}) %collective-permute-start.33) | collective-permute-done | bytes 524320 | tf_op jit(solution)/shard_map/ppermute | solution.py:38
  227.0 9.2 %collective-permute-done.27.refs_6_ = bf16[4,4,128,128]{3,2,1,0:T(8,128)(2,1)} collective-permute-done((bf16[4,4,128,128]{3,2,1,0:T(8,128)(2,1)}, bf16[4,4,128,128]{3,2,1,0:T(8,128)(2,1)}, u32[]{:S(2)}, u32[]{:S(2)}) %collective-permute-start.27) | collective-permute-done | bytes 524320 | tf_op jit(solution)/shard_map/ppermute | solution.py:43
  236.2 5.8 %sum_blocks.3 = (f32[8,128,256]{2,1,0:T(8,128)}, f32[8,128,256]{2,1,0:T(8,128)}) custom-call(s32[4]{0:T(128)} %pad_add_fusion.2.pos_ref, s32[64]{0:T(128)} %reshape.130.ids_ref, bf16[4,4,128,128]{3,2,1,0:T(8,128)(2,1)} %get-tuple-element.50.refs_0_, bf16[4,4,128,128]{3,2,1,0:T(8,128)(2,1)} %copy-done.9, bf16[4,4,128,128]{3,2,1,0:T(8,128)(2,1)} %copy-done.10, ...), custom_call_target="tpu_custom_call" | custom-call | flops 2097152 | bytes 12582912 | tf_op jit(solution)/shard_map/sum_blocks/pallas_call | solution.py:177
  258.1 28.0 %collective-permute-done.37.refs_7_ = f32[256,256]{1,0:T(8,128)S(1)} collective-permute-done((f32[256,256]{1,0:T(8,128)S(1)}, f32[256,256]{1,0:T(8,128)S(1)}, u32[]{:S(2)}, u32[]{:S(2)}) %collective-permute-start.37) | collective-permute-done | bytes 262176 | tf_op jit(solution)/shard_map/ppermute | solution.py:48
  287.5 6.6 %label_side.1 = (bf16[256,768]{1,0:T(8,128)(2,1)}, bf16[256,2048]{1,0:T(8,128)(2,1)}, bf16[256,768]{1,0:T(8,128)(2,1)}) custom-call(f32[256,512]{1,0:T(8,128)} %bitcast.77, f32[256,512]{1,0:T(8,128)} %copy-done.14, f32[256,512]{1,0:T(8,128)} %copy-done.12, f32[256,512]{1,0:T(8,128)} %copy-done.13, f32[256,256]{1,0:T(8,128)} %bitcast.78, ...), custom_call_target="tpu_custom_call" | custom-call | tf_op jit(solution)/shard_map/label_side/pallas_call | solution.py:214
  295.6 132.1 %all-gather.5.cloned.1.call-done = bf16[32768,768]{1,0:T(8,128)(2,1)} async-done(((bf16[256,768]{1,0:T(8,128)(2,1)}), bf16[32768,768]{1,0:T(8,128)(2,1)}) %all-gather.5.cloned.1.call-update) | async-done | bytes 50331664 | tf_op jit(solution)/shard_map/all_gather | solution.py:328
  427.7 12.6 %target_blocks.1 = bf16[16,128,768]{2,1,0:T(8,128)(2,1)} custom-call(s32[1]{0:T(128)} %bitcast.28.count_ref, s32[64]{0:T(128)} %get-tuple-element.71.slot_ref, s32[64]{0:T(128)} %get-tuple-element.70.inst_ref, s32[64]{0:T(128)} %get-tuple-element.69.lab_ref, s32[64,128,128]{2,1,0:T(8,128)} %bitcast.58, s32[64,128,128]{2,1,0:T(8,128)} %bitcast.59, ...), custom_call_target="tpu_custom_call" | custom-call | tf_op jit(solution)/shard_map/target_blocks/pallas_call | solution.py:268
  (151 shorter events, 92.5 us)
Async XLA Ops:
  7.2 279.0 %all-gather.3.cloned.1.call-start = ((), (), s32[]{:S(2)}) async-start(), calls=%async_computation | async-start | bytes 3170304 | tf_op jit(solution)/shard_map/all_gather | solution.py:304
  18.3 41.8 %collective-permute-start.7 = (bf16[4,4,128,256]{3,2,1,0:T(8,128)(2,1)}, bf16[4,4,128,256]{3,2,1,0:T(8,128)(2,1)S(1)}, u32[]{:S(2)}, u32[]{:S(2)}) collective-permute-start(bf16[4,4,128,256]{3,2,1,0:T(8,128)(2,1)} %get-tuple-element.37), channel_id=1, source_target_pairs={{0,8},{1,9},{2,10},{3,11},{4,12},{5,13},{6,14},{7,15},{8,0},{9,1},... | collective-permute-start | bytes 3145736 | tf_op jit(solution)/shard_map/ppermute | solution.py:38
  18.8 47.2 %collective-permute-start.8 = (bf16[4,4,128,256]{3,2,1,0:T(8,128)(2,1)}, bf16[4,4,128,256]{3,2,1,0:T(8,128)(2,1)S(1)}, u32[]{:S(2)}, u32[]{:S(2)}) collective-permute-start(bf16[4,4,128,256]{3,2,1,0:T(8,128)(2,1)} %get-tuple-element.38), channel_id=1, source_target_pairs={{0,12},{1,13},{2,14},{3,15},{4,0},{5,1},{6,2},{7,3},{8,4},{9,5},{1... | collective-permute-start | bytes 3145736 | tf_op jit(solution)/shard_map/ppermute | solution.py:38
  20.3 407.4 %all-gather.5.cloned.1.call-start = ((), (), s32[]{:S(2)}) async-start(), calls=%async_computation.1 | async-start | bytes 50724864 | tf_op jit(solution)/shard_map/all_gather | solution.py:328
  24.0 77.7 %collective-permute-start.12 = (bf16[4,4,128,256]{3,2,1,0:T(8,128)(2,1)}, bf16[4,4,128,256]{3,2,1,0:T(8,128)(2,1)}, u32[]{:S(2)}, u32[]{:S(2)}) collective-permute-start(bf16[4,4,128,256]{3,2,1,0:T(8,128)(2,1)} %partial_blocks.11), channel_id=1, source_target_pairs={{0,1},{1,2},{2,3},{3,0},{4,5},{5,6},{6,7},{7,4},{8,9},{9,10},{10,1... | collective-permute-start | bytes 3145736 | tf_op jit(solution)/shard_map/ppermute | solution.py:43
  28.5 73.3 %collective-permute-start.13 = (bf16[4,4,128,256]{3,2,1,0:T(8,128)(2,1)}, bf16[4,4,128,256]{3,2,1,0:T(8,128)(2,1)}, u32[]{:S(2)}, u32[]{:S(2)}) collective-permute-start(bf16[4,4,128,256]{3,2,1,0:T(8,128)(2,1)} %get-tuple-element.43), channel_id=1, source_target_pairs={{0,2},{1,3},{2,0},{3,1},{4,6},{5,7},{6,4},{7,5},{8,10},{9,11},{10,... | collective-permute-start | bytes 3145736 | tf_op jit(solution)/shard_map/ppermute | solution.py:43
  37.4 65.8 %collective-permute-start.14 = (bf16[4,4,128,256]{3,2,1,0:T(8,128)(2,1)}, bf16[4,4,128,256]{3,2,1,0:T(8,128)(2,1)}, u32[]{:S(2)}, u32[]{:S(2)}) collective-permute-start(bf16[4,4,128,256]{3,2,1,0:T(8,128)(2,1)} %get-tuple-element.44), channel_id=1, source_target_pairs={{0,3},{1,0},{2,1},{3,2},{4,7},{5,4},{6,5},{7,6},{8,11},{9,8},{10,9... | collective-permute-start | bytes 3145736 | tf_op jit(solution)/shard_map/ppermute | solution.py:43
  71.0 62.7 %collective-permute-start.9 = (bf16[4,4,128,256]{3,2,1,0:T(8,128)(2,1)}, bf16[4,4,128,256]{3,2,1,0:T(8,128)(2,1)S(1)}, u32[]{:S(2)}, u32[]{:S(2)}) collective-permute-start(bf16[4,4,128,256]{3,2,1,0:T(8,128)(2,1)} %get-tuple-element.39), channel_id=1, source_target_pairs={{0,1},{1,2},{2,3},{3,0},{4,5},{5,6},{6,7},{7,4},{8,9},{9,10},{10,1... | collective-permute-start | bytes 3145736 | tf_op jit(solution)/shard_map/ppermute | solution.py:43
  101.8 31.1 %collective-permute-start.30 = (bf16[4,4,128,128]{3,2,1,0:T(8,128)(2,1)}, bf16[4,4,128,128]{3,2,1,0:T(8,128)(2,1)S(1)}, u32[]{:S(2)}, u32[]{:S(2)}) collective-permute-start(bf16[4,4,128,128]{3,2,1,0:T(8,128)(2,1)} %get-tuple-element.60), channel_id=1, source_target_pairs={{0,3},{1,0},{2,1},{3,2},{4,7},{5,4},{6,5},{7,6},{8,11},{9,8},{10,9... | collective-permute-start | bytes 1572872 | tf_op jit(solution)/shard_map/ppermute | solution.py:43
  103.2 48.2 %collective-permute-start.10 = (bf16[4,4,128,256]{3,2,1,0:T(8,128)(2,1)}, bf16[4,4,128,256]{3,2,1,0:T(8,128)(2,1)}, u32[]{:S(2)}, u32[]{:S(2)}) collective-permute-start(bf16[4,4,128,256]{3,2,1,0:T(8,128)(2,1)} %get-tuple-element.40), channel_id=1, source_target_pairs={{0,2},{1,3},{2,0},{3,1},{4,6},{5,7},{6,4},{7,5},{8,10},{9,11},{10,... | collective-permute-start | bytes 3145736 | tf_op jit(solution)/shard_map/ppermute | solution.py:43
  116.2 59.7 %collective-permute-start.11 = (bf16[4,4,128,256]{3,2,1,0:T(8,128)(2,1)}, bf16[4,4,128,256]{3,2,1,0:T(8,128)(2,1)}, u32[]{:S(2)}, u32[]{:S(2)}) collective-permute-start(bf16[4,4,128,256]{3,2,1,0:T(8,128)(2,1)} %get-tuple-element.41), channel_id=1, source_target_pairs={{0,3},{1,0},{2,1},{3,2},{4,7},{5,4},{6,5},{7,6},{8,11},{9,8},{10,9... | collective-permute-start | bytes 3145736 | tf_op jit(solution)/shard_map/ppermute | solution.py:43
  117.3 60.1 %collective-permute-start.15 = (bf16[4,4,128,256]{3,2,1,0:T(8,128)(2,1)}, bf16[4,4,128,256]{3,2,1,0:T(8,128)(2,1)}, u32[]{:S(2)}, u32[]{:S(2)}) collective-permute-start(bf16[4,4,128,256]{3,2,1,0:T(8,128)(2,1)} %get-tuple-element.45), channel_id=1, source_target_pairs={{0,4},{1,5},{2,6},{3,7},{4,8},{5,9},{6,10},{7,11},{8,12},{9,13},{1... | collective-permute-start | bytes 3145736 | tf_op jit(solution)/shard_map/ppermute | solution.py:38
  133.0 49.5 %collective-permute-start.16 = (bf16[4,4,128,256]{3,2,1,0:T(8,128)(2,1)}, bf16[4,4,128,256]{3,2,1,0:T(8,128)(2,1)}, u32[]{:S(2)}, u32[]{:S(2)}) collective-permute-start(bf16[4,4,128,256]{3,2,1,0:T(8,128)(2,1)} %get-tuple-element.46), channel_id=1, source_target_pairs={{0,8},{1,9},{2,10},{3,11},{4,12},{5,13},{6,14},{7,15},{8,0},{9,1},... | collective-permute-start | bytes 3145736 | tf_op jit(solution)/shard_map/ppermute | solution.py:38
  133.7 48.8 %collective-permute-start.17 = (bf16[4,4,128,256]{3,2,1,0:T(8,128)(2,1)}, bf16[4,4,128,256]{3,2,1,0:T(8,128)(2,1)}, u32[]{:S(2)}, u32[]{:S(2)}) collective-permute-start(bf16[4,4,128,256]{3,2,1,0:T(8,128)(2,1)} %get-tuple-element.47), channel_id=1, source_target_pairs={{0,12},{1,13},{2,14},{3,15},{4,0},{5,1},{6,2},{7,3},{8,4},{9,5},{1... | collective-permute-start | bytes 3145736 | tf_op jit(solution)/shard_map/ppermute | solution.py:38
  151.5 40.9 %collective-permute-start.22 = (bf16[4,4,128,128]{3,2,1,0:T(8,128)(2,1)}, bf16[4,4,128,128]{3,2,1,0:T(8,128)(2,1)S(1)}, u32[]{:S(2)}, u32[]{:S(2)}) collective-permute-start(bf16[4,4,128,128]{3,2,1,0:T(8,128)(2,1)} %get-tuple-element.51), channel_id=1, source_target_pairs={{0,4},{1,5},{2,6},{3,7},{4,8},{5,9},{6,10},{7,11},{8,12},{9,13},{1... | collective-permute-start | bytes 1572872 | tf_op jit(solution)/shard_map/ppermute | solution.py:38
  176.0 28.4 %collective-permute-start.23 = (bf16[4,4,128,128]{3,2,1,0:T(8,128)(2,1)}, bf16[4,4,128,128]{3,2,1,0:T(8,128)(2,1)S(1)}, u32[]{:S(2)}, u32[]{:S(2)}) collective-permute-start(bf16[4,4,128,128]{3,2,1,0:T(8,128)(2,1)} %get-tuple-element.52), channel_id=1, source_target_pairs={{0,8},{1,9},{2,10},{3,11},{4,12},{5,13},{6,14},{7,15},{8,0},{9,1},... | collective-permute-start | bytes 1572872 | tf_op jit(solution)/shard_map/ppermute | solution.py:38
  177.3 30.2 %collective-permute-start.24 = (bf16[4,4,128,128]{3,2,1,0:T(8,128)(2,1)}, bf16[4,4,128,128]{3,2,1,0:T(8,128)(2,1)}, u32[]{:S(2)}, u32[]{:S(2)}) collective-permute-start(bf16[4,4,128,128]{3,2,1,0:T(8,128)(2,1)} %get-tuple-element.53), channel_id=1, source_target_pairs={{0,12},{1,13},{2,14},{3,15},{4,0},{5,1},{6,2},{7,3},{8,4},{9,5},{1... | collective-permute-start | bytes 1572872 | tf_op jit(solution)/shard_map/ppermute | solution.py:38
  182.5 30.3 %collective-permute-start.32 = (bf16[4,4,128,128]{3,2,1,0:T(8,128)(2,1)}, bf16[4,4,128,128]{3,2,1,0:T(8,128)(2,1)}, u32[]{:S(2)}, u32[]{:S(2)}) collective-permute-start(bf16[4,4,128,128]{3,2,1,0:T(8,128)(2,1)} %get-tuple-element.62), channel_id=1, source_target_pairs={{0,8},{1,9},{2,10},{3,11},{4,12},{5,13},{6,14},{7,15},{8,0},{9,1},... | collective-permute-start | bytes 1572872 | tf_op jit(solution)/shard_map/ppermute | solution.py:38
  192.4 57.5 %collective-permute-start.18 = (f32[8,128,512]{2,1,0:T(8,128)}, f32[8,128,512]{2,1,0:T(8,128)S(1)}, u32[]{:S(2)}, u32[]{:S(2)}) collective-permute-start(f32[8,128,512]{2,1,0:T(8,128)} %get-tuple-element.49), channel_id=1, source_target_pairs={{0,16},{16,0},{32,48},{48,32},{64,80},{80,64},{96,112},{112,96},{1... | collective-permute-start | bytes 6291464 | tf_op jit(solution)/shard_map/ppermute | solution.py:52
  251.1 35.0 %collective-permute-start.20 = (f32[256,512]{1,0:T(8,128)S(1)}, f32[256,512]{1,0:T(8,128)S(1)}, u32[]{:S(2)}, u32[]{:S(2)}) collective-permute-start(f32[256,512]{1,0:T(8,128)S(1)} %bitcast.81), channel_id=1, source_target_pairs={{0,64},{16,80},{32,96},{48,112},{64,0},{80,16},{96,32},{112,48},{1... | collective-permute-start | bytes 1572872 | tf_op jit(solution)/shard_map/ppermute | solution.py:48
  252.6 33.6 %collective-permute-start.21 = (f32[256,512]{1,0:T(8,128)S(1)}, f32[256,512]{1,0:T(8,128)S(1)}, u32[]{:S(2)}, u32[]{:S(2)}) collective-permute-start(f32[256,512]{1,0:T(8,128)S(1)} %bitcast.80), channel_id=1, source_target_pairs={{0,96},{16,112},{32,0},{48,16},{64,32},{80,48},{96,64},{112,80},{1... | collective-permute-start | bytes 1572872 | tf_op jit(solution)/shard_map/ppermute | solution.py:48
  252.6 33.6 %collective-permute-start.19 = (f32[256,512]{1,0:T(8,128)S(1)}, f32[256,512]{1,0:T(8,128)S(1)}, u32[]{:S(2)}, u32[]{:S(2)}) collective-permute-start(f32[256,512]{1,0:T(8,128)S(1)} %bitcast.79), channel_id=1, source_target_pairs={{0,32},{16,48},{32,64},{48,80},{64,96},{80,112},{96,0},{112,16},{1... | collective-permute-start | bytes 1572872 | tf_op jit(solution)/shard_map/ppermute | solution.py:48
  254.0 32.1 %collective-permute-start.37 = (f32[256,256]{1,0:T(8,128)S(1)}, f32[256,256]{1,0:T(8,128)S(1)}, u32[]{:S(2)}, u32[]{:S(2)}) collective-permute-start(f32[256,256]{1,0:T(8,128)S(1)} %bitcast.83), channel_id=1, source_target_pairs={{0,96},{16,112},{32,0},{48,16},{64,32},{80,48},{96,64},{112,80},{1... | collective-permute-start | bytes 786440 | tf_op jit(solution)/shard_map/ppermute | solution.py:48
  257.4 28.8 %collective-permute-start.35 = (f32[256,256]{1,0:T(8,128)S(1)}, f32[256,256]{1,0:T(8,128)S(1)}, u32[]{:S(2)}, u32[]{:S(2)}) collective-permute-start(f32[256,256]{1,0:T(8,128)S(1)} %bitcast.82), channel_id=1, source_target_pairs={{0,32},{16,48},{32,64},{48,80},{64,96},{80,112},{96,0},{112,16},{1... | collective-permute-start | bytes 786440 | tf_op jit(solution)/shard_map/ppermute | solution.py:48
  (39 other events, 428.3 us)
Sparse Core Ops, SparseCore 0:
  20.4 104.3 all-gather.2
  294.2 133.4 all-gather.4

commit v3 on v2

--- a/solution.py
+++ b/solution.py
@@ -18,12 +18,12 @@
 
 
 MAKE = (
-    (0, ((0, 1),)),
-    (0, ((1, 1),)),
-    (0, ((0, 3), (0, 2))),
-    (0, ((1, 3), (1, 2))),
-    (1, ((0, 1), (0, 3), (0, 2))),
-    (1, ((1, 1), (1, 3), (1, 2))),
+    (0, ((0, 2),)),
+    (0, ((1, 2),)),
+    (0, ((0, 1), (0, 3))),
+    (0, ((1, 1), (1, 3))),
+    (1, ((0, 2), (0, 1), (0, 3))),
+    (1, ((1, 2), (1, 1), (1, 3))),
     (0, ((0, 0), (1, 0))),
     (1, ((0, 0), (1, 0))),
 )
@@ -142,13 +142,11 @@
         sender = step[0] * SIDE + step[1]
         for k in range(cap):
             target = ids_ref[sender * cap + k]
-
-            @pl.when(target >= 0)
-            def _():
-                away = jnp.bitwise_xor(jnp.bitwise_and(target >> 1, 1), pos_ref[3])
-                row = away * half + mod4((target >> 2) - pos_ref[2]) * LB_DEV + jnp.bitwise_and(target, 1)
-                columns = pl.ds(first_axis * width, width)
-                total[row, :, columns] += ref[row_at, k].astype(jnp.float32)
+            away = jnp.bitwise_xor(jnp.bitwise_and(target >> 1, 1), pos_ref[3])
+            row = away * half + mod4((target >> 2) - pos_ref[2]) * LB_DEV + jnp.bitwise_and(target, 1)
+            row = jnp.where(target >= 0, row, 2 * half)
+            columns = pl.ds(first_axis * width, width)
+            total[row, :, columns] += ref[row_at, k].astype(jnp.float32)
 
     for first_axis in range(2):
         refs_here = arrived[first_axis * (2 * SIDE - 1) : (first_axis + 1) * (2 * SIDE - 1)]
@@ -165,7 +163,7 @@
     @pl.when(at == SIDE - per_step)
     def _():
         keep_ref[...] = total[:half]
-        send_ref[...] = total[half:]
+        send_ref[...] = total[half : 2 * half]
 
 
 def sum_blocks(pos, flat_ids, arrived, col_blocks):
@@ -182,7 +180,7 @@
             grid=(SUM_STEPS,),
             in_specs=([own] * SIDE + [far] * (SIDE - 1)) * 2,
             out_specs=(whole, whole),
-            scratch_shapes=[pltpu.VMEM((col_blocks, block, 2 * width), jnp.float32)],
+            scratch_shapes=[pltpu.VMEM((col_blocks + 1, block, 2 * width), jnp.float32)],
         ),
         cost_estimate=pl.CostEstimate(
             flops=SIDE * SIDE * cap * block * 2 * width, bytes_accessed=12 << 20, transcendentals=0
@@ -297,7 +295,6 @@
     near = [shift_first(tagged_ids[step], step) if step else tagged_ids[0] for step in range(SIDE)]
     near = jnp.stack(near, axis=1)
     near = [shift_second(near[step], step) if step else near[0] for step in range(SIDE)]
-    flat_ids = jnp.stack(near, axis=1).reshape(-1)
 
     share = centroids.shape[0] // planes
     own_rows = lax.dynamic_slice_in_dim(centroids, d * share, share, 0)
@@ -318,6 +315,9 @@
             packed = pack_groups(received)
             for outer, group in enumerate(packed, start=1):
                 arrived.append(shifts[1 - first_axis](group, outer))
+        if part == 0:
+            near, arrived = lax.optimization_barrier((near, arrived))
+            flat_ids = jnp.stack(near, axis=1).reshape(-1)
         keep, send = sum_blocks(pos, flat_ids, arrived, planes * LB_DEV)
         other = swap_core(send)
         for step in range(SIDE):

time: 451 us -> 457 us (1.013)
  waiting for transfers between devices: 272 us -> 283 us
  starting transfers between devices: 69.8 us -> 64.9 us
    ppermute x15, starting transfers between devices: 23.1 us -> 35.6 us  [shift_second(): return lax.ppermute(array, 'label', pairs)]
    ppermute x2, starting transfers between devices: 13.7 us -> 3.13 us  [swap_core(): lax.ppermute(array, 'dp', [(a * 2 + b, a * 2 + 1 - b) for a in range(SIDE...]
    ppermute x15, waiting for transfers between devices: 44.8 us -> 53.8 us  [shift_first(): return lax.ppermute(array, 'label', pairs)]
    ppermute x15, starting transfers between devices: 26.7 us -> 21.4 us  [shift_first(): return lax.ppermute(array, 'label', pairs)]
  transfers between devices with their start and end apart: 40 -> 40, of which waited for: 20 -> 21; matrix products, arithmetic and copies ran while one was open for 2% -> 2% of each run, Pallas kernels for 13% -> 12%
where the time goes in v3:
time: 457 us; the launch traced here: 453 us
  waiting for transfers between devices  283 us (62%)
  Pallas kernels  78.8 us (17%)
  starting transfers between devices  64.9 us (14%)
  between operations  14.3 us (3%)
  local copies, waits for them, and re-layouts  6.25 us (1%)
  other arithmetic  5.66 us (1%)
    all_gather x1, waiting for transfers between devices, body(): mixed_all = lax.all_gather(mixed, ('dp', 'label'), axis=0, tiled=True)  132 us
    ppermute x15, waiting for transfers between devices, shift_second(): return lax.ppermute(array, 'label', pairs)  62.3 us
    ppermute x15, waiting for transfers between devices, shift_first(): return lax.ppermute(array, 'label', pairs)  53.8 us
    ppermute x15, starting transfers between devices, shift_second(): return lax.ppermute(array, 'label', pairs)  35.6 us
    pallas_call x8, Pallas kernels, partial_blocks(): pl.pallas_call(functools.partial(partial_kernel, cap, groups, axes), out_...  33.2 us
    ppermute x6, waiting for transfers between devices, shift_plane(): return lax.ppermute(array, 'dp', pairs)  31.9 us
    ppermute x15, starting transfers between devices, shift_first(): return lax.ppermute(array, 'label', pairs)  21.4 us
    pallas_call x4, Pallas kernels, pack_groups(): pl.pallas_call(pack_kernel, out_shape=(jax.ShapeDtypeStruct(shape, receiv...  13.2 us
  transfers between devices with their start and end apart: 40, of which 21 were waited for; matrix products, arithmetic and copies ran while one was open for 2% of the time, Pallas kernels for 12%

profile of v3, /device:TPU:61, one launch (start us, length us, event | category | flops | bytes accessed | tf_op | source)
XLA Modules:
  0.0 452.7 jit_solution(12365774875084287493)
XLA Ops:
  13.2 4.4 partial_blocks.9
  24.8 4.3 partial_blocks.11
  31.7 4.7 %partial_blocks.8 = (bf16[4,4,128,256]{3,2,1,0:T(8,128)(2,1)}, bf16[4,4,128,256]{3,2,1,0:T(8,128)(2,1)}) custom-call(s32[4]{0:T(128)} %pad_add_fusion.2.pos_ref, s32[64]{0:T(128)} %reshape.130.inst_ref, s32[4,4,4,128,128]{4,3,2,1,0:T(8,128)} %bitcast.49, s32[4,4,4,128,128]{4,3,2,1,0:T(8,128)} %bitcast.50, bf16[16,128,768]{2,1,0:T(8,128)(2,1)} %bitcast.71, ...), custom_call_target="tpu_custom_call" | custom-call | flops 268435456 | bytes 8388608 | tf_op jit(solution)/shard_map/partial_blocks/pallas_call | solution.py:91
  39.5 23.1 %collective-permute-done.6.refs_1_ = bf16[4,4,128,256]{3,2,1,0:T(8,128)(2,1)S(1)} collective-permute-done((bf16[4,4,128,256]{3,2,1,0:T(8,128)(2,1)}, bf16[4,4,128,256]{3,2,1,0:T(8,128)(2,1)S(1)}, u32[]{:S(2)}, u32[]{:S(2)}) %collective-permute-start.6) | collective-permute-done | bytes 1048608 | tf_op jit(solution)/shard_map/ppermute | solution.py:38
  63.9 3.9 pack_groups.4
  82.0 17.6 %collective-permute-start.5 = (s32[4,4]{1,0:T(4,128)S(1)}, s32[4,4]{1,0:T(4,128)S(1)}, u32[]{:S(2)}, u32[]{:S(2)}) collective-permute-start(s32[4,4]{1,0:T(4,128)S(1)} %bitcast.97), channel_id=1, source_target_pairs={{0,3},{1,0},{2,1},{3,2},{4,7},{5,4},{6,5},{7,6},{8,11},{9,8},{10,9... | collective-permute-start | bytes 200 | tf_op jit(solution)/shard_map/ppermute | solution.py:43
  102.5 4.3 partial_blocks.15
  111.8 3.9 pack_groups.5
  120.3 17.7 %collective-permute-done.30.refs_3_.refs_10_ = bf16[4,4,128,128]{3,2,1,0:T(8,128)(2,1)S(1)} collective-permute-done((bf16[4,4,128,128]{3,2,1,0:T(8,128)(2,1)}, bf16[4,4,128,128]{3,2,1,0:T(8,128)(2,1)S(1)}, u32[]{:S(2)}, u32[]{:S(2)}) %collective-permute-start.30) | collective-permute-done | bytes 524320 | tf_op jit(solution)/shard_map/ppermute | solution.py:43
  141.6 4.3 partial_blocks.14
  145.8 6.2 %collective-permute-done.10.refs_5_ = bf16[4,4,128,256]{3,2,1,0:T(8,128)(2,1)} collective-permute-done((bf16[4,4,128,256]{3,2,1,0:T(8,128)(2,1)}, bf16[4,4,128,256]{3,2,1,0:T(8,128)(2,1)}, u32[]{:S(2)}, u32[]{:S(2)}) %collective-permute-start.10) | collective-permute-done | bytes 1048608 | tf_op jit(solution)/shard_map/ppermute | solution.py:43
  154.1 3.9 partial_blocks.13
  158.1 20.7 %collective-permute-done.11.refs_6_ = bf16[4,4,128,256]{3,2,1,0:T(8,128)(2,1)} collective-permute-done((bf16[4,4,128,256]{3,2,1,0:T(8,128)(2,1)}, bf16[4,4,128,256]{3,2,1,0:T(8,128)(2,1)}, u32[]{:S(2)}, u32[]{:S(2)}) %collective-permute-start.11) | collective-permute-done | bytes 1048608 | tf_op jit(solution)/shard_map/ppermute | solution.py:43
  188.7 7.8 %sum_blocks.2 = (f32[8,128,512]{2,1,0:T(8,128)}, f32[8,128,512]{2,1,0:T(8,128)}) custom-call(s32[4]{0:T(128)} %pad_add_fusion.2.pos_ref, s32[64]{0:T(128)} %reshape.133.ids_ref, bf16[4,4,128,256]{3,2,1,0:T(8,128)(2,1)} %get-tuple-element.70.refs_0_, bf16[4,4,128,256]{3,2,1,0:T(8,128)(2,1)} %copy-done.3, bf16[4,4,128,256]{3,2,1,0:T(8,128)(2,1)} %copy-done.2, ...), custom_call_target="tpu_custom_call" | custom-call | flops 4194304 | bytes 12582912 | tf_op jit(solution)/shard_map/sum_blocks/pallas_call | solution.py:175
  200.9 8.7 %collective-permute-done.24.refs_3_ = bf16[4,4,128,128]{3,2,1,0:T(8,128)(2,1)} collective-permute-done((bf16[4,4,128,128]{3,2,1,0:T(8,128)(2,1)}, bf16[4,4,128,128]{3,2,1,0:T(8,128)(2,1)}, u32[]{:S(2)}, u32[]{:S(2)}) %collective-permute-start.24) | collective-permute-done | bytes 524320 | tf_op jit(solution)/shard_map/ppermute | solution.py:38
  212.3 4.1 collective-permute-start.25
  218.5 13.0 %collective-permute-done.33.refs_13_ = bf16[4,4,128,128]{3,2,1,0:T(8,128)(2,1)} collective-permute-done((bf16[4,4,128,128]{3,2,1,0:T(8,128)(2,1)}, bf16[4,4,128,128]{3,2,1,0:T(8,128)(2,1)}, u32[]{:S(2)}, u32[]{:S(2)}) %collective-permute-start.33) | collective-permute-done | bytes 524320 | tf_op jit(solution)/shard_map/ppermute | solution.py:38
  231.6 5.8 %collective-permute-done.25.refs_4_ = bf16[4,4,128,128]{3,2,1,0:T(8,128)(2,1)S(1)} collective-permute-done((bf16[4,4,128,128]{3,2,1,0:T(8,128)(2,1)}, bf16[4,4,128,128]{3,2,1,0:T(8,128)(2,1)S(1)}, u32[]{:S(2)}, u32[]{:S(2)}) %collective-permute-start.25) | collective-permute-done | bytes 524320 | tf_op jit(solution)/shard_map/ppermute | solution.py:43
  237.3 5.9 %collective-permute-done.27.refs_6_ = bf16[4,4,128,128]{3,2,1,0:T(8,128)(2,1)} collective-permute-done((bf16[4,4,128,128]{3,2,1,0:T(8,128)(2,1)}, bf16[4,4,128,128]{3,2,1,0:T(8,128)(2,1)}, u32[]{:S(2)}, u32[]{:S(2)}) %collective-permute-start.27) | collective-permute-done | bytes 524320 | tf_op jit(solution)/shard_map/ppermute | solution.py:43
  243.2 5.3 %sum_blocks.3 = (f32[8,128,256]{2,1,0:T(8,128)}, f32[8,128,256]{2,1,0:T(8,128)}) custom-call(s32[4]{0:T(128)} %pad_add_fusion.2.pos_ref, s32[64]{0:T(128)} %reshape.133.ids_ref, bf16[4,4,128,128]{3,2,1,0:T(8,128)(2,1)} %get-tuple-element.86.refs_0_, bf16[4,4,128,128]{3,2,1,0:T(8,128)(2,1)} %copy-done.9, bf16[4,4,128,128]{3,2,1,0:T(8,128)(2,1)} %copy-done.10, ...), custom_call_target="tpu_custom_call" | custom-call | flops 2097152 | bytes 12582912 | tf_op jit(solution)/shard_map/sum_blocks/pallas_call | solution.py:175
  262.7 28.8 %collective-permute-done.37.refs_7_ = f32[256,256]{1,0:T(8,128)S(1)} collective-permute-done((f32[256,256]{1,0:T(8,128)S(1)}, f32[256,256]{1,0:T(8,128)S(1)}, u32[]{:S(2)}, u32[]{:S(2)}) %collective-permute-start.37) | collective-permute-done | bytes 262176 | tf_op jit(solution)/shard_map/ppermute | solution.py:48
  292.8 6.6 %label_side.1 = (bf16[256,768]{1,0:T(8,128)(2,1)}, bf16[256,2048]{1,0:T(8,128)(2,1)}, bf16[256,768]{1,0:T(8,128)(2,1)}) custom-call(f32[256,512]{1,0:T(8,128)} %bitcast.78, f32[256,512]{1,0:T(8,128)} %copy-done.14, f32[256,512]{1,0:T(8,128)} %copy-done.12, f32[256,512]{1,0:T(8,128)} %copy-done.13, f32[256,256]{1,0:T(8,128)} %bitcast.79, ...), custom_call_target="tpu_custom_call" | custom-call | tf_op jit(solution)/shard_map/label_side/pallas_call | solution.py:212
  301.0 132.2 %all-gather.5.cloned.1.call-done = bf16[32768,768]{1,0:T(8,128)(2,1)} async-done(((bf16[256,768]{1,0:T(8,128)(2,1)}), bf16[32768,768]{1,0:T(8,128)(2,1)}) %all-gather.5.cloned.1.call-update) | async-done | bytes 50331664 | tf_op jit(solution)/shard_map/all_gather | solution.py:328
  433.2 12.6 %target_blocks.1 = bf16[16,128,768]{2,1,0:T(8,128)(2,1)} custom-call(s32[1]{0:T(128)} %bitcast.29.count_ref, s32[64]{0:T(128)} %get-tuple-element.107.slot_ref, s32[64]{0:T(128)} %get-tuple-element.106.inst_ref, s32[64]{0:T(128)} %get-tuple-element.105.lab_ref, s32[64,128,128]{2,1,0:T(8,128)} %bitcast.59, s32[64,128,128]{2,1,0:T(8,128)} %bitcast.60, ...), custom_call_target="tpu_custom_call" | custom-call | tf_op jit(solution)/shard_map/target_blocks/pallas_call | solution.py:266
  (151 shorter events, 88.6 us)
Async XLA Ops:
  7.2 284.4 %all-gather.3.cloned.1.call-start = ((), (), s32[]{:S(2)}) async-start(), calls=%async_computation | async-start | bytes 3170304 | tf_op jit(solution)/shard_map/all_gather | solution.py:301
  17.6 45.0 %collective-permute-start.6 = (bf16[4,4,128,256]{3,2,1,0:T(8,128)(2,1)}, bf16[4,4,128,256]{3,2,1,0:T(8,128)(2,1)S(1)}, u32[]{:S(2)}, u32[]{:S(2)}) collective-permute-start(bf16[4,4,128,256]{3,2,1,0:T(8,128)(2,1)} %get-tuple-element.55), channel_id=1, source_target_pairs={{0,4},{1,5},{2,6},{3,7},{4,8},{5,9},{6,10},{7,11},{8,12},{9,13},{1... | collective-permute-start | bytes 3145736 | tf_op jit(solution)/shard_map/ppermute | solution.py:38
  19.4 43.2 %collective-permute-start.8 = (bf16[4,4,128,256]{3,2,1,0:T(8,128)(2,1)}, bf16[4,4,128,256]{3,2,1,0:T(8,128)(2,1)S(1)}, u32[]{:S(2)}, u32[]{:S(2)}) collective-permute-start(bf16[4,4,128,256]{3,2,1,0:T(8,128)(2,1)} %get-tuple-element.56), channel_id=1, source_target_pairs={{0,12},{1,13},{2,14},{3,15},{4,0},{5,1},{6,2},{7,3},{8,4},{9,5},{1... | collective-permute-start | bytes 3145736 | tf_op jit(solution)/shard_map/ppermute | solution.py:38
  20.1 413.1 %all-gather.5.cloned.1.call-start = ((), (), s32[]{:S(2)}) async-start(), calls=%async_computation.1 | async-start | bytes 50724864 | tf_op jit(solution)/shard_map/all_gather | solution.py:328
  23.8 83.1 %collective-permute-start.13 = (bf16[4,4,128,256]{3,2,1,0:T(8,128)(2,1)}, bf16[4,4,128,256]{3,2,1,0:T(8,128)(2,1)}, u32[]{:S(2)}, u32[]{:S(2)}) collective-permute-start(bf16[4,4,128,256]{3,2,1,0:T(8,128)(2,1)} %partial_blocks.12), channel_id=1, source_target_pairs={{0,2},{1,3},{2,0},{3,1},{4,6},{5,7},{6,4},{7,5},{8,10},{9,11},{10,... | collective-permute-start | bytes 3145736 | tf_op jit(solution)/shard_map/ppermute | solution.py:43
  29.1 79.5 %collective-permute-start.12 = (bf16[4,4,128,256]{3,2,1,0:T(8,128)(2,1)}, bf16[4,4,128,256]{3,2,1,0:T(8,128)(2,1)}, u32[]{:S(2)}, u32[]{:S(2)}) collective-permute-start(bf16[4,4,128,256]{3,2,1,0:T(8,128)(2,1)} %get-tuple-element.61), channel_id=1, source_target_pairs={{0,1},{1,2},{2,3},{3,0},{4,5},{5,6},{6,7},{7,4},{8,9},{9,10},{10,1... | collective-permute-start | bytes 3145736 | tf_op jit(solution)/shard_map/ppermute | solution.py:43
  39.0 70.0 %collective-permute-start.14 = (bf16[4,4,128,256]{3,2,1,0:T(8,128)(2,1)}, bf16[4,4,128,256]{3,2,1,0:T(8,128)(2,1)}, u32[]{:S(2)}, u32[]{:S(2)}) collective-permute-start(bf16[4,4,128,256]{3,2,1,0:T(8,128)(2,1)} %get-tuple-element.62), channel_id=1, source_target_pairs={{0,3},{1,0},{2,1},{3,2},{4,7},{5,4},{6,5},{7,6},{8,11},{9,8},{10,9... | collective-permute-start | bytes 3145736 | tf_op jit(solution)/shard_map/ppermute | solution.py:43
  67.9 73.7 %collective-permute-start.9 = (bf16[4,4,128,256]{3,2,1,0:T(8,128)(2,1)}, bf16[4,4,128,256]{3,2,1,0:T(8,128)(2,1)S(1)}, u32[]{:S(2)}, u32[]{:S(2)}) collective-permute-start(bf16[4,4,128,256]{3,2,1,0:T(8,128)(2,1)} %get-tuple-element.57), channel_id=1, source_target_pairs={{0,1},{1,2},{2,3},{3,0},{4,5},{5,6},{6,7},{7,4},{8,9},{9,10},{10,1... | collective-permute-start | bytes 3145736 | tf_op jit(solution)/shard_map/ppermute | solution.py:43
  108.6 29.3 %collective-permute-start.30 = (bf16[4,4,128,128]{3,2,1,0:T(8,128)(2,1)}, bf16[4,4,128,128]{3,2,1,0:T(8,128)(2,1)S(1)}, u32[]{:S(2)}, u32[]{:S(2)}) collective-permute-start(bf16[4,4,128,128]{3,2,1,0:T(8,128)(2,1)} %get-tuple-element.96), channel_id=1, source_target_pairs={{0,3},{1,0},{2,1},{3,2},{4,7},{5,4},{6,5},{7,6},{8,11},{9,8},{10,9... | collective-permute-start | bytes 1572872 | tf_op jit(solution)/shard_map/ppermute | solution.py:43
  108.9 43.1 %collective-permute-start.10 = (bf16[4,4,128,256]{3,2,1,0:T(8,128)(2,1)}, bf16[4,4,128,256]{3,2,1,0:T(8,128)(2,1)}, u32[]{:S(2)}, u32[]{:S(2)}) collective-permute-start(bf16[4,4,128,256]{3,2,1,0:T(8,128)(2,1)} %get-tuple-element.58), channel_id=1, source_target_pairs={{0,2},{1,3},{2,0},{3,1},{4,6},{5,7},{6,4},{7,5},{8,10},{9,11},{10,... | collective-permute-start | bytes 3145736 | tf_op jit(solution)/shard_map/ppermute | solution.py:43
  117.5 61.2 %collective-permute-start.11 = (bf16[4,4,128,256]{3,2,1,0:T(8,128)(2,1)}, bf16[4,4,128,256]{3,2,1,0:T(8,128)(2,1)}, u32[]{:S(2)}, u32[]{:S(2)}) collective-permute-start(bf16[4,4,128,256]{3,2,1,0:T(8,128)(2,1)} %get-tuple-element.59), channel_id=1, source_target_pairs={{0,3},{1,0},{2,1},{3,2},{4,7},{5,4},{6,5},{7,6},{8,11},{9,8},{10,9... | collective-permute-start | bytes 3145736 | tf_op jit(solution)/shard_map/ppermute | solution.py:43
  118.2 64.0 %collective-permute-start.15 = (bf16[4,4,128,256]{3,2,1,0:T(8,128)(2,1)}, bf16[4,4,128,256]{3,2,1,0:T(8,128)(2,1)}, u32[]{:S(2)}, u32[]{:S(2)}) collective-permute-start(bf16[4,4,128,256]{3,2,1,0:T(8,128)(2,1)} %get-tuple-element.63), channel_id=1, source_target_pairs={{0,4},{1,5},{2,6},{3,7},{4,8},{5,9},{6,10},{7,11},{8,12},{9,13},{1... | collective-permute-start | bytes 3145736 | tf_op jit(solution)/shard_map/ppermute | solution.py:38
  137.9 47.0 %collective-permute-start.16 = (bf16[4,4,128,256]{3,2,1,0:T(8,128)(2,1)}, bf16[4,4,128,256]{3,2,1,0:T(8,128)(2,1)}, u32[]{:S(2)}, u32[]{:S(2)}) collective-permute-start(bf16[4,4,128,256]{3,2,1,0:T(8,128)(2,1)} %get-tuple-element.64), channel_id=1, source_target_pairs={{0,8},{1,9},{2,10},{3,11},{4,12},{5,13},{6,14},{7,15},{8,0},{9,1},... | collective-permute-start | bytes 3145736 | tf_op jit(solution)/shard_map/ppermute | solution.py:38
  141.5 45.6 %collective-permute-start.17 = (bf16[4,4,128,256]{3,2,1,0:T(8,128)(2,1)}, bf16[4,4,128,256]{3,2,1,0:T(8,128)(2,1)}, u32[]{:S(2)}, u32[]{:S(2)}) collective-permute-start(bf16[4,4,128,256]{3,2,1,0:T(8,128)(2,1)} %get-tuple-element.65), channel_id=1, source_target_pairs={{0,12},{1,13},{2,14},{3,15},{4,0},{5,1},{6,2},{7,3},{8,4},{9,5},{1... | collective-permute-start | bytes 3145736 | tf_op jit(solution)/shard_map/ppermute | solution.py:38
  152.1 44.4 %collective-permute-start.22 = (bf16[4,4,128,128]{3,2,1,0:T(8,128)(2,1)}, bf16[4,4,128,128]{3,2,1,0:T(8,128)(2,1)S(1)}, u32[]{:S(2)}, u32[]{:S(2)}) collective-permute-start(bf16[4,4,128,128]{3,2,1,0:T(8,128)(2,1)} %get-tuple-element.87), channel_id=1, source_target_pairs={{0,4},{1,5},{2,6},{3,7},{4,8},{5,9},{6,10},{7,11},{8,12},{9,13},{1... | collective-permute-start | bytes 1572872 | tf_op jit(solution)/shard_map/ppermute | solution.py:38
  184.9 31.4 %collective-permute-start.31 = (bf16[4,4,128,128]{3,2,1,0:T(8,128)(2,1)}, bf16[4,4,128,128]{3,2,1,0:T(8,128)(2,1)}, u32[]{:S(2)}, u32[]{:S(2)}) collective-permute-start(bf16[4,4,128,128]{3,2,1,0:T(8,128)(2,1)} %get-tuple-element.97), channel_id=1, source_target_pairs={{0,4},{1,5},{2,6},{3,7},{4,8},{5,9},{6,10},{7,11},{8,12},{9,13},{1... | collective-permute-start | bytes 1572872 | tf_op jit(solution)/shard_map/ppermute | solution.py:38
  187.1 30.6 %collective-permute-start.32 = (bf16[4,4,128,128]{3,2,1,0:T(8,128)(2,1)}, bf16[4,4,128,128]{3,2,1,0:T(8,128)(2,1)}, u32[]{:S(2)}, u32[]{:S(2)}) collective-permute-start(bf16[4,4,128,128]{3,2,1,0:T(8,128)(2,1)} %get-tuple-element.98), channel_id=1, source_target_pairs={{0,8},{1,9},{2,10},{3,11},{4,12},{5,13},{6,14},{7,15},{8,0},{9,1},... | collective-permute-start | bytes 1572872 | tf_op jit(solution)/shard_map/ppermute | solution.py:38
  196.5 57.2 %collective-permute-start.18 = (f32[8,128,512]{2,1,0:T(8,128)}, f32[8,128,512]{2,1,0:T(8,128)S(1)}, u32[]{:S(2)}, u32[]{:S(2)}) collective-permute-start(f32[8,128,512]{2,1,0:T(8,128)} %get-tuple-element.85), channel_id=1, source_target_pairs={{0,16},{16,0},{32,48},{48,32},{64,80},{80,64},{96,112},{112,96},{1... | collective-permute-start | bytes 6291464 | tf_op jit(solution)/shard_map/ppermute | solution.py:52
  199.0 32.5 %collective-permute-start.33 = (bf16[4,4,128,128]{3,2,1,0:T(8,128)(2,1)}, bf16[4,4,128,128]{3,2,1,0:T(8,128)(2,1)}, u32[]{:S(2)}, u32[]{:S(2)}) collective-permute-start(bf16[4,4,128,128]{3,2,1,0:T(8,128)(2,1)} %get-tuple-element.99), channel_id=1, source_target_pairs={{0,12},{1,13},{2,14},{3,15},{4,0},{5,1},{6,2},{7,3},{8,4},{9,5},{1... | collective-permute-start | bytes 1572872 | tf_op jit(solution)/shard_map/ppermute | solution.py:38
  254.9 36.5 %collective-permute-start.20 = (f32[256,512]{1,0:T(8,128)S(1)}, f32[256,512]{1,0:T(8,128)S(1)}, u32[]{:S(2)}, u32[]{:S(2)}) collective-permute-start(f32[256,512]{1,0:T(8,128)S(1)} %bitcast.82), channel_id=1, source_target_pairs={{0,64},{16,80},{32,96},{48,112},{64,0},{80,16},{96,32},{112,48},{1... | collective-permute-start | bytes 1572872 | tf_op jit(solution)/shard_map/ppermute | solution.py:48
  257.9 33.6 %collective-permute-start.21 = (f32[256,512]{1,0:T(8,128)S(1)}, f32[256,512]{1,0:T(8,128)S(1)}, u32[]{:S(2)}, u32[]{:S(2)}) collective-permute-start(f32[256,512]{1,0:T(8,128)S(1)} %bitcast.81), channel_id=1, source_target_pairs={{0,96},{16,112},{32,0},{48,16},{64,32},{80,48},{96,64},{112,80},{1... | collective-permute-start | bytes 1572872 | tf_op jit(solution)/shard_map/ppermute | solution.py:48
  258.1 33.4 %collective-permute-start.19 = (f32[256,512]{1,0:T(8,128)S(1)}, f32[256,512]{1,0:T(8,128)S(1)}, u32[]{:S(2)}, u32[]{:S(2)}) collective-permute-start(f32[256,512]{1,0:T(8,128)S(1)} %bitcast.80), channel_id=1, source_target_pairs={{0,32},{16,48},{32,64},{48,80},{64,96},{80,112},{96,0},{112,16},{1... | collective-permute-start | bytes 1572872 | tf_op jit(solution)/shard_map/ppermute | solution.py:48
  259.4 32.1 %collective-permute-start.37 = (f32[256,256]{1,0:T(8,128)S(1)}, f32[256,256]{1,0:T(8,128)S(1)}, u32[]{:S(2)}, u32[]{:S(2)}) collective-permute-start(f32[256,256]{1,0:T(8,128)S(1)} %bitcast.84), channel_id=1, source_target_pairs={{0,96},{16,112},{32,0},{48,16},{64,32},{80,48},{96,64},{112,80},{1... | collective-permute-start | bytes 786440 | tf_op jit(solution)/shard_map/ppermute | solution.py:48
  262.7 28.8 %collective-permute-start.35 = (f32[256,256]{1,0:T(8,128)S(1)}, f32[256,256]{1,0:T(8,128)S(1)}, u32[]{:S(2)}, u32[]{:S(2)}) collective-permute-start(f32[256,256]{1,0:T(8,128)S(1)} %bitcast.83), channel_id=1, source_target_pairs={{0,32},{16,48},{32,64},{48,80},{64,96},{80,112},{96,0},{112,16},{1... | collective-permute-start | bytes 786440 | tf_op jit(solution)/shard_map/ppermute | solution.py:48
  (39 other events, 433.3 us)
Sparse Core Ops, SparseCore 0:
  20.2 81.0 all-gather.2
  299.6 133.5 all-gather.4
